TPU v7x, 128 devices: a whole 4x4x4 slice. The times are simulated.
128 devices in a mesh: region: 8 (over x, core), dom: 16 (over y, z).
Axes of the slice: x: 4, y: 4, z: 4, core: 2. Of those that a mesh axis runs over, the one named last changes fastest.
Arguments:
- embeds: bfloat16 [262144, 256], P(('region', 'dom')), may hold values from -6 to 6
- neighbours: int32 [262144, 8], P(('region', 'dom')), may hold values from 0 to 4095
- halo_send: int32 [2048, 128], P(('region', 'dom')), may hold values from 0 to 2047
- gnn_weight: bfloat16 [512, 256], replicated, may hold values from -0.25 to 0.25
- pair_local: int32 [1024, 512], P(('region', 'dom')), may hold values from 0 to 2047
- pair_remote: int32 [1024, 512], P(('region', 'dom')), may hold values from 0 to 2047
- pair_count: int32 [128, 8], P(('region', 'dom')), may hold values from 1 to 512, as said below
- targets: float32 [1024, 512], P(('region', 'dom')), may hold values from -6 to 6
- pair_w1: bfloat16 [512, 256], replicated, may hold values from -0.25 to 0.25
- pair_w2: bfloat16 [256], replicated, may hold values from -0.375 to 0.375
Outputs:
- embeds_grad: bfloat16 [262144, 256], P(('region', 'dom'))
- gnn_grad: float32 [512, 256], replicated
- pair_w1_grad: float32 [512, 256], replicated
- pair_w2_grad: float32 [256], replicated
- loss: float32 [], replicated
Inputs may be any that keep to these rules, and one draw needn't show every extreme that they name: `pair_count`: some partition has 512 live slots for some owner region in every draw.
All inputs are finite; a program needn't handle non-finite values.
Results may differ from a plain program's by a relative error of at most 0.0061.
Values may be sent and summed in bfloat16 or wider, within the bound.
A program may use at most 128 MiB of HBM per device.

v0:
```python
import jax
import jax.numpy as jnp
from jax import lax
from jax.sharding import PartitionSpec as P

gelu_coef = 0.7978845608


def gelu_tanh(value):
    inner = jnp.tanh(gelu_coef * (value + 0.044715 * value * value * value))
    return 0.5 * value * (1.0 + inner)


def gelu_slope(value):
    inner = jnp.tanh(gelu_coef * (value + 0.044715 * value * value * value))
    return 0.5 * (1.0 + inner) + 0.5 * value * (1.0 - inner * inner) * gelu_coef * (
        1.0 + 3.0 * 0.044715 * value * value
    )


def local(
    embeds,
    neighbours,
    halo_send,
    gnn_weight,
    pair_local,
    pair_remote,
    pair_count,
    targets,
    pair_w1,
    pair_w2,
):
    net_rows = embeds.shape[0]
    feat_width = embeds.shape[1]
    degree = neighbours.shape[1]
    regions = pair_local.shape[0]
    slot_cap = pair_local.shape[1]
    peers = halo_send.shape[0]
    halo_rows = halo_send.shape[1]
    table_rows = net_rows + peers * halo_rows
    nets_total = net_rows * lax.axis_size("region") * lax.axis_size("dom")
    contract_rows = (((0,), (0,)), ((), ()))
    contract_cols = (((1,), (1,)), ((), ()))
    net_ids = jnp.arange(net_rows, dtype=jnp.int32)
    selector = (halo_send.reshape(-1)[:, None] == net_ids[None, :]).astype(jnp.bfloat16)
    outgoing = (
        jnp.dot(selector, embeds, preferred_element_type=jnp.float32)
        .astype(jnp.bfloat16)
        .reshape(peers, halo_rows, feat_width)
    )
    received = lax.all_to_all(outgoing, "dom", split_axis=0, concat_axis=0, tiled=True)
    table = jnp.concatenate([embeds, received.reshape(-1, feat_width)], 0)
    table_ids = jnp.arange(table_rows, dtype=jnp.int32)
    adjacency = jnp.zeros((net_rows, table_rows), jnp.bfloat16)
    for column in range(degree):
        adjacency = adjacency + (neighbours[:, column][:, None] == table_ids[None, :]).astype(
            jnp.bfloat16
        )
    agg_sum = jnp.dot(adjacency, table, preferred_element_type=jnp.float32)
    aggregate = (agg_sum / degree).astype(jnp.bfloat16)
    joined = jnp.concatenate([embeds, aggregate], 1)
    pre = jnp.dot(joined, gnn_weight, preferred_element_type=jnp.float32)
    nets = (embeds.astype(jnp.float32) + gelu_tanh(pre)).astype(jnp.bfloat16)
    local_count = jnp.sum(pair_count).astype(jnp.float32)
    total_count = lax.psum(local_count, ("region", "dom"))
    asked = lax.all_to_all(pair_remote, "region", split_axis=0, concat_axis=0, tiled=True)
    partner = lax.all_to_all(nets[asked], "region", split_axis=0, concat_axis=0, tiled=True)
    victim = nets[pair_local]
    pairs_in = jnp.concatenate([victim, partner], 2).reshape(regions * slot_cap, 2 * feat_width)
    linear = jnp.dot(pairs_in, pair_w1, preferred_element_type=jnp.float32)
    activated = gelu_tanh(linear).astype(jnp.bfloat16)
    scores = jnp.dot(activated, pair_w2, preferred_element_type=jnp.float32)
    slot_ids = jnp.arange(slot_cap, dtype=jnp.int32)
    valid_mask = (
        (slot_ids[None, :] < pair_count.reshape(-1)[:, None]).astype(jnp.float32).reshape(-1)
    )
    errors = (scores - targets.reshape(-1)) * valid_mask
    sq_local = jnp.sum(errors * errors)
    residual = 2.0 * errors
    lin_grad = (
        residual[:, None] * pair_w2.astype(jnp.float32)[None, :] * gelu_slope(linear)
    ).astype(jnp.bfloat16)
    grad_w1 = lax.dot_general(pairs_in, lin_grad, contract_rows, preferred_element_type=jnp.float32)
    grad_w2 = jnp.sum(residual[:, None] * activated.astype(jnp.float32), 0)
    pair_grad = lax.dot_general(
        lin_grad, pair_w1, contract_cols, preferred_element_type=jnp.float32
    )
    victim_grad = pair_grad[:, :feat_width]
    partner_grad = (
        pair_grad[:, feat_width:].astype(jnp.bfloat16).reshape(regions, slot_cap, feat_width)
    )
    nets_grad = (
        jnp.zeros((net_rows, feat_width), jnp.float32).at[pair_local.reshape(-1)].add(victim_grad)
    )
    returned_pairs = lax.all_to_all(partner_grad, "region", split_axis=0, concat_axis=0, tiled=True)
    nets_grad = nets_grad.at[asked.reshape(-1)].add(
        returned_pairs.reshape(-1, feat_width).astype(jnp.float32)
    )
    pre_grad = (nets_grad * gelu_slope(pre)).astype(jnp.bfloat16)
    grad_gnn = lax.dot_general(joined, pre_grad, contract_rows, preferred_element_type=jnp.float32)
    cat_grad = lax.dot_general(
        pre_grad, gnn_weight, contract_cols, preferred_element_type=jnp.float32
    )
    agg_grad = (cat_grad[:, feat_width:] / degree).astype(jnp.bfloat16)
    table_grad = lax.dot_general(
        adjacency, agg_grad, contract_rows, preferred_element_type=jnp.float32
    )
    halo_back = table_grad[net_rows:].astype(jnp.bfloat16).reshape(peers, halo_rows, feat_width)
    returned_halo = lax.all_to_all(halo_back, "dom", split_axis=0, concat_axis=0, tiled=True)
    embeds_sum = nets_grad + cat_grad[:, :feat_width] + table_grad[:net_rows]
    embeds_sum = embeds_sum + lax.dot_general(
        selector,
        returned_halo.reshape(-1, feat_width),
        contract_rows,
        preferred_element_type=jnp.float32,
    )
    gnn_sum, w1_sum, w2_sum, sq_sum = lax.psum(
        (grad_gnn, grad_w1, grad_w2, sq_local), ("region", "dom")
    )
    root_count = jnp.sqrt(total_count)
    embeds_grad = (embeds_sum * (8.0 * nets_total / total_count)).astype(jnp.bfloat16)
    return (
        embeds_grad,
        8.0 * gnn_sum / root_count,
        8.0 * w1_sum / root_count,
        8.0 * w2_sum / root_count,
        sq_sum / total_count,
    )


def solution(mesh):
    in_specs = (
        P(("region", "dom"), None),
        P(("region", "dom"), None),
        P(("region", "dom"), None),
        P(),
        P(("region", "dom"), None),
        P(("region", "dom"), None),
        P(("region", "dom"), None),
        P(("region", "dom"), None),
        P(),
        P(),
    )
    out_specs = (P(("region", "dom"), None), P(), P(), P(), P())
    return jax.shard_map(local, mesh=mesh, in_specs=in_specs, out_specs=out_specs, check_vma=False)
```

profile of v0, /device:TPU:1, one launch (start us, length us, event | category | flops | bytes accessed | tf_op | source)
XLA Modules:
  0.0 452.1 jit_solution(9494208046124771384)
XLA Ops:
  8.6 5.8 %all-to-all-start.1 = ((s32[8,1,512]{2,1,0:T(1,128)}), s32[8,1,512]{2,1,0:T(1,128)S(1)}, u32[]{:S(2)}, u32[]{:S(2)}) async-start(s32[8,1,512]{2,1,0:T(1,128)} %all_to_all.21), calls=%async_computation.1 | async-start | bytes 32768 | tf_op jit(solution)/shard_map/all_to_all | solution.py:66
  14.3 5.1 %fusion.40 = bf16[2048,256]{1,0:T(8,128)(2,1)} fusion(bf16[2048,256]{1,0:T(8,128)(2,1)} %param.10, s32[2048]{0:T(1024)} %bitcast.87), kind=kOutput, calls=%fused_computation.57 | convolution fusion | flops 2152202240 | bytes 2105344 | tf_op jit(solution)/shard_map/dot_general | solution.py:47
  19.5 7.9 %all-to-all-start = ((bf16[16,128,256]{2,1,0:T(8,128)(2,1)}), bf16[16,128,256]{2,1,0:T(8,128)(2,1)S(1)}, u32[]{:S(2)}, u32[]{:S(2)}) async-start(bf16[16,128,256]{2,1,0:T(8,128)(2,1)} %bitcast.11), calls=%async_computation | async-start | bytes 2097152 | tf_op jit(solution)/shard_map/all_to_all | solution.py:51
  28.8 14.8 %all-to-all-done = bf16[16,128,256]{2,1,0:T(8,128)(2,1)S(1)} async-done(((bf16[16,128,256]{2,1,0:T(8,128)(2,1)}), bf16[16,128,256]{2,1,0:T(8,128)(2,1)S(1)}, u32[]{:S(2)}, u32[]{:S(2)}) %all-to-all-start) | async-done | bytes 1048608 | tf_op jit(solution)/shard_map/all_to_all | solution.py:51
  43.6 50.0 %fusion.41 = bf16[2048,256]{0,1:T(8,128)(2,1)} fusion(s32[2048]{0:T(1024)S(1)} %bitcast.82, s32[2048]{0:T(1024)} %bitcast.84, s32[2048]{0:T(1024)S(1)} %bitcast.72, s32[2048]{0:T(1024)S(1)} %bitcast.74, s32[2048]{0:T(1024)S(1)} %bitcast.76, s32[2048]{0:T(1024)S(1)} %bitcast.78, s32[2048]{0:T(1024)S(1)} %bitcast.80, s32[2048]{0:T(1024)S(1)} %bitcast.70, ...), kind=kOutput, calls=%fused_computation.58 | convolution fusion | flops 4568645632 | bytes 3211264 | tf_op jit(solution)/shard_map/dot_general | solution.py:59
  93.6 3.7 add_convert_fusion
  97.4 17.0 %gather_fusion.1 = bf16[4096,256]{1,0:T(8,128)(2,1)} fusion(bf16[2048,256]{1,0:T(8,128)(2,1)S(1)} %get-tuple-element.22, s32[4096]{0:T(1024)S(1)} %broadcast_clamp_fusion), kind=kCustom, calls=%fused_computation.1 | custom fusion | bytes 4210688 | tf_op jit(solution)/shard_map/gather | solution.py:67
  114.4 7.1 %all-to-all-start.2 = ((bf16[8,512,256]{2,1,0:T(8,128)(2,1)}), bf16[8,512,256]{2,1,0:T(8,128)(2,1)S(1)}, u32[]{:S(2)}, u32[]{:S(2)}) async-start(bf16[8,512,256]{2,1,0:T(8,128)(2,1)} %bitcast.54), calls=%async_computation.2 | async-start | bytes 4194304 | tf_op jit(solution)/shard_map/all_to_all | solution.py:67
  122.2 17.0 %gather_fusion = bf16[4096,256]{1,0:T(8,128)(2,1)} fusion(bf16[2048,256]{1,0:T(8,128)(2,1)S(1)} %get-tuple-element.22, s32[4096]{0:T(1024)S(1)} %broadcast_clamp_fusion.1), kind=kCustom, calls=%fused_computation | custom fusion | bytes 4210688 | tf_op jit(solution)/shard_map/gather | solution.py:68
  139.2 8.4 %all-to-all-done.2 = bf16[8,512,256]{2,1,0:T(8,128)(2,1)S(1)} async-done(((bf16[8,512,256]{2,1,0:T(8,128)(2,1)}), bf16[8,512,256]{2,1,0:T(8,128)(2,1)S(1)}, u32[]{:S(2)}, u32[]{:S(2)}) %all-to-all-start.2) | async-done | bytes 2097184 | tf_op jit(solution)/shard_map/all_to_all | solution.py:67
  152.8 3.3 multiply_reduce_fusion
  157.4 3.2 copy-done.1
  162.2 5.2 %all-to-all-start.3 = ((bf16[8,512,256]{2,1,0:T(8,128)(2,1)}), bf16[8,512,256]{2,1,0:T(8,128)(2,1)}, u32[]{:S(2)}, u32[]{:S(2)}) async-start(bf16[8,512,256]{2,1,0:T(8,128)(2,1)} %bitcast.53), calls=%async_computation.3 | async-start | bytes 4194304 | tf_op jit(solution)/shard_map/all_to_all | solution.py:95
  167.4 24.5 %scatter_custom_fusion = f32[2048,256]{1,0:T(8,128)} fusion(s32[4096]{0:T(1024)S(1)} %bitcast.68, f32[4096,512]{1,0:T(8,128)} %copy-done.1, f32[]{:T(128)} %constant.12.clone.1), kind=kCustom, calls=%fused_computation.44 | custom fusion | flops 1048576 | bytes 6291968 | tf_op jit(solution)/shard_map/scatter-add | solution.py:93
  192.0 4.3 fusion.68
  196.3 26.2 %scatter_custom_fusion.1 = f32[2048,256]{1,0:T(8,128)} fusion(f32[2048,256]{1,0:T(8,128)} %scatter_custom_fusion, s32[4096]{0:T(1024)S(1)} %bitcast.67, bf16[4096,256]{1,0:T(8,128)(2,1)} %bitcast.25), kind=kCustom, calls=%fused_computation.47 | custom fusion | flops 2097152 | bytes 4194304 | tf_op jit(solution)/shard_map/scatter-add | solution.py:96
  222.5 3.0 fusion.50
  230.2 39.3 %fusion.19 = f32[4096,256]{1,0:T(8,128)S(1)} fusion(s32[2048]{0:T(1024)S(1)} %bitcast.83, s32[2048]{0:T(1024)S(1)} %bitcast.85, s32[2048]{0:T(1024)S(1)} %bitcast.73, s32[2048]{0:T(1024)S(1)} %bitcast.75, s32[2048]{0:T(1024)S(1)} %bitcast.77, s32[2048]{0:T(1024)S(1)} %bitcast.79, s32[2048]{0:T(1024)S(1)} %bitcast.81, s32[2048]{0:T(1024)S(1)} %bitcast.71, ...), kind=kOutput, calls=%fused_computation.32 | convolution fusion | flops 4564451328 | bytes 6356992 | tf_op jit(solution)/shard_map/dot_general | solution.py:105
  272.6 4.4 all-to-all-start.4
  277.1 3.2 fusion.54
  281.6 68.0 %all-reduce = (f32[]{:T(128)}, f32[256]{0:T(256)S(1)}, f32[]{:T(128)}) all-reduce(f32[]{:T(128)S(6)} %convert_element_type.90, f32[256]{0:T(256)S(1)} %get-tuple-element.20, f32[]{:T(128)} %get-tuple-element.18), channel_id=1, replica_groups=mesh['region'=8,'dom'=16] {'region','dom'}, use_global_device_ids=true, to_apply=%region_3.0 | all-reduce | flops 258 | bytes 2064 | tf_op jit(solution)/shard_map/psum | solution.py:65
  352.9 80.3 %all-reduce.4.cloned.1.call-done = (f32[512,256]{1,0:T(8,128)}, f32[512,256]{1,0:T(8,128)}) async-done(((f32[512,256]{1,0:T(8,128)}, f32[512,256]{1,0:T(8,128)}), (f32[512,256]{1,0:T(8,128)}, f32[512,256]{1,0:T(8,128)})) %all-reduce.4.cloned.1.call-update) | async-done | bytes 1048592 | tf_op jit(solution)/shard_map/psum | solution.py:117
  433.2 2.3 multiply_divide_fusion
  435.4 8.5 %fusion.39 = bf16[2048,256]{1,0:T(8,128)(2,1)} fusion(bf16[2048,256]{1,0:T(8,128)(2,1)} %bitcast.24, s32[2048]{0:T(1024)S(1)} %bitcast.88, f32[4096,256]{1,0:T(8,128)} %copy-done.9, f32[2048,256]{1,0:T(8,128)S(1)} %copy-done.3, f32[2048,512]{1,0:T(8,128)} %copy-done.2, f32[]{:T(128)S(6)} %div.30), kind=kOutput, calls=%fused_computation.56 | convolution fusion | flops 2154299392 | bytes 8396804 | tf_op jit(solution)/shard_map/dot_general | solution.py:111
  (70 shorter events, 20.7 us)
Async XLA Ops:
  7.2 142.4 %copy-start = (bf16[512,256]{1,0:T(8,128)(2,1)S(1)}, bf16[512,256]{1,0:T(8,128)(2,1)}, u32[]{:S(2)}) copy-start(bf16[512,256]{1,0:T(8,128)(2,1)} %param.18) | copy-start | bytes 786436
  8.6 10.9 %all-to-all-start.1 = ((s32[8,1,512]{2,1,0:T(1,128)}), s32[8,1,512]{2,1,0:T(1,128)S(1)}, u32[]{:S(2)}, u32[]{:S(2)}) async-start(s32[8,1,512]{2,1,0:T(1,128)} %all_to_all.21), calls=%async_computation.1 | async-start | bytes 32768 | tf_op jit(solution)/shard_map/all_to_all | solution.py:66
  14.3 13.0 %copy-start.6 = (bf16[2048,256]{1,0:T(8,128)(2,1)S(1)}, bf16[2048,256]{1,0:T(8,128)(2,1)}, u32[]{:S(2)}) copy-start(bf16[2048,256]{1,0:T(8,128)(2,1)} %param.10) | copy-start | bytes 3145732
  19.5 8.6 %copy-start.10 = (s32[2048,8]{0,1:T(8,128)S(1)}, s32[2048,8]{0,1:T(8,128)}, u32[]{:S(2)}) copy-start(s32[2048,8]{0,1:T(8,128)} %param.11) | copy-start | bytes 196612
  19.5 24.2 %all-to-all-start = ((bf16[16,128,256]{2,1,0:T(8,128)(2,1)}), bf16[16,128,256]{2,1,0:T(8,128)(2,1)S(1)}, u32[]{:S(2)}, u32[]{:S(2)}) async-start(bf16[16,128,256]{2,1,0:T(8,128)(2,1)} %bitcast.11), calls=%async_computation | async-start | bytes 2097152 | tf_op jit(solution)/shard_map/all_to_all | solution.py:51
  28.1 65.6 %copy-start.7 = (bf16[2048,256]{0,1:T(8,128)(2,1)}, bf16[2048,256]{0,1:T(8,128)(2,1)S(1)}, u32[]{:S(2)}) copy-start(bf16[2048,256]{0,1:T(8,128)(2,1)S(1)} %copy.17) | copy-start | bytes 3145732
  114.3 7.1 %copy-start.18 = (bf16[256]{0:T(256)(128)(2,1)S(1)}, bf16[256]{0:T(256)(128)(2,1)}, u32[]{:S(2)}) copy-start(bf16[256]{0:T(256)(128)(2,1)} %param.19) | copy-start | bytes 1540
  114.3 7.7 %copy-start.15 = (s32[1,8]{1,0:T(1,128)S(1)}, s32[1,8]{1,0:T(1,128)}, u32[]{:S(2)}) copy-start(s32[1,8]{1,0:T(1,128)} %param.16) | copy-start | bytes 100
  114.3 7.7 %copy-start.12 = (f32[8,512]{1,0:T(8,128)S(1)}, f32[8,512]{1,0:T(8,128)}, u32[]{:S(2)}) copy-start(f32[8,512]{1,0:T(8,128)} %param.17) | copy-start | bytes 49156
  114.3 7.8 %copy-start.11 = (s32[8,512]{1,0:T(8,128)S(1)}, s32[8,512]{1,0:T(8,128)}, u32[]{:S(2)}) copy-start(s32[8,512]{1,0:T(8,128)} %param.14) | copy-start | bytes 49156
  114.4 33.3 %all-to-all-start.2 = ((bf16[8,512,256]{2,1,0:T(8,128)(2,1)}), bf16[8,512,256]{2,1,0:T(8,128)(2,1)S(1)}, u32[]{:S(2)}, u32[]{:S(2)}) async-start(bf16[8,512,256]{2,1,0:T(8,128)(2,1)} %bitcast.54), calls=%async_computation.2 | async-start | bytes 4194304 | tf_op jit(solution)/shard_map/all_to_all | solution.py:67
  149.6 2.0 copy-start.4
  149.6 2.0 copy-start.14
  157.4 3.2 copy-start.1
  162.2 34.1 %all-to-all-start.3 = ((bf16[8,512,256]{2,1,0:T(8,128)(2,1)}), bf16[8,512,256]{2,1,0:T(8,128)(2,1)}, u32[]{:S(2)}, u32[]{:S(2)}) async-start(bf16[8,512,256]{2,1,0:T(8,128)(2,1)} %bitcast.53), calls=%async_computation.3 | async-start | bytes 4194304 | tf_op jit(solution)/shard_map/all_to_all | solution.py:95
  196.3 26.2 %copy-start.5 = (f32[2048,256]{1,0:T(8,128)S(1)}, f32[2048,256]{1,0:T(8,128)}, u32[]{:S(2)}) copy-start(f32[2048,256]{1,0:T(8,128)} %get-tuple-element.23) | copy-start | bytes 6291460
  222.5 3.0 copy-start.8
  228.1 2.1 copy-start.13
  269.6 2.0 copy-start.9
  272.6 162.8 %all-to-all-start.4 = ((bf16[16,128,256]{2,1,0:T(8,128)(2,1)}), bf16[16,128,256]{2,1,0:T(8,128)(2,1)}, u32[]{:S(2)}, u32[]{:S(2)}) async-start(bf16[16,128,256]{2,1,0:T(8,128)(2,1)} %bitcast.23), calls=%async_computation.4 | async-start | bytes 2097152 | tf_op jit(solution)/shard_map/all_to_all | solution.py:109
  277.0 3.3 copy-start.16
  277.0 158.4 %copy-start.3 = (f32[2048,256]{1,0:T(8,128)S(1)}, f32[2048,256]{1,0:T(8,128)}, u32[]{:S(2)}) copy-start(f32[2048,256]{1,0:T(8,128)} %scatter_custom_fusion.1) | copy-start | bytes 6291460
  277.0 158.4 %copy-start.17 = (s32[16,128]{1,0:T(8,128)S(1)}, s32[16,128]{1,0:T(8,128)}, u32[]{:S(2)}) copy-start(s32[16,128]{1,0:T(8,128)} %param.12) | copy-start | bytes 24580
  277.0 156.1 %all-reduce.4.cloned.1.call-start = ((), (), s32[]{:S(2)}) async-start(), calls=%async_computation.5 | async-start | bytes 2097152 | tf_op jit(solution)/shard_map/psum | solution.py:117
  (1 other events, 1.9 us)
Sparse Core Ops, SparseCore 0:
  283.4 149.7 all-reduce.3
where the time goes:
time: 456 us; the launch traced here: 452 us
  matrix products  118 us (26%)
  waiting for transfers between devices  104 us (23%)
  blocking collectives  68 us (15%)
  other arithmetic  63.1 us (14%)
  local copies, waits for them, and re-layouts  49.6 us (11%)
  starting transfers between devices  30.3 us (7%)
  between operations  19.1 us (4%)
    psum x1, waiting for transfers between devices, local(): lax.psum((grad_gnn, grad_w1, grad_w2, sq_local), ('region', 'dom'))  80.3 us
    psum x1, blocking collectives, local(): total_count = lax.psum(local_count, ('region', 'dom'))  68 us
    dot_general x1, matrix products, local(): agg_sum = jnp.dot(adjacency, table, preferred_element_type=jnp.float32)  50 us
    dot_general x1, matrix products, local(): lax.dot_general(adjacency, agg_grad, contract_rows, preferred_element_typ...  39.3 us
    scatter-add x1, other arithmetic, local(): nets_grad.at[asked.reshape(-1)]  26.2 us
    scatter-add x1, other arithmetic, local(): jnp.zeros((net_rows, feat_width), jnp.float32).at[pair_local.reshape(-1)]  24.5 us
    gather x1, local copies, waits for them, and re-layouts, local(): victim = nets[pair_local]  17 us
    gather x1, local copies, waits for them, and re-layouts, local(): nets[asked]  17 us
  transfers between devices with their start and end apart: 6, of which 3 were waited for; matrix products, arithmetic and copies ran while one was open for 13% of the time, Pallas kernels for 0%

commit v1 on v0

v1 whole, which is shorter than its diff:
```python
import functools
import jax
import jax.numpy as jnp
from jax import lax
from jax.sharding import PartitionSpec as P
from jax.experimental import pallas as pl
from jax.experimental.pallas import tpu as pltpu

f32 = jnp.float32
bf16 = jnp.bfloat16
gelu_coef = 0.7978845608
contract_rows = (((0,), (0,)), ((), ()))
contract_cols = (((1,), (1,)), ((), ()))
VMEM_LIMIT = 60 * 1024 * 1024
FIELDS = 8


def gelu_both(value):
    inner = jnp.tanh(gelu_coef * (value + 0.044715 * value * value * value))
    half = 0.5 * (1.0 + inner)
    slope = half + 0.5 * value * (1.0 - inner * inner) * gelu_coef * (
        1.0 + 3.0 * 0.044715 * value * value
    )
    return value * half, slope


def gelu_slope(value):
    return gelu_both(value)[1]


def dot(a, b):
    return jnp.dot(a, b, preferred_element_type=f32)


def call(body, outs, grid, in_specs, out_specs, scratch=(), flops=0, nbytes=0, name=None):
    return pl.pallas_call(
        body,
        out_shape=outs,
        grid=grid,
        in_specs=in_specs,
        out_specs=out_specs,
        scratch_shapes=list(scratch),
        name=name,
        cost_estimate=pl.CostEstimate(flops=flops, bytes_accessed=nbytes, transcendentals=0),
        compiler_params=pltpu.CompilerParams(
            dimension_semantics=("arbitrary",) * len(grid), vmem_limit_bytes=VMEM_LIMIT
        ),
    )


def whole(shape):
    zero = (0,) * len(shape)
    return pl.BlockSpec(shape, lambda *_: zero)


def field_scale(field):
    return -(16.0 ** -field) if field == FIELDS - 1 else 16.0 ** -field


def field_mask(field):
    mask = 15 << (4 * field)
    return mask - (1 << 32) if mask >= (1 << 31) else mask


def expand(words, field):
    return (words & field_mask(field)).astype(f32).astype(bf16)


def agg_own_body(nb_ref, table_ref, words_ref, sum_ref, scaled):
    width = words_ref.shape[1]
    half = FIELDS // 2

    @pl.when(pl.program_id(0) == 0)
    def _():
        for field in range(half):
            scaled[field * width:(field + 1) * width, :] = (
                table_ref[field * width:(field + 1) * width, :].astype(f32) * field_scale(field)
            ).astype(bf16)

    nb = nb_ref[...]
    low = nb & (width - 1)
    shift = 4 * (nb >> (width.bit_length() - 1))
    weight = jnp.where(shift == 4 * (FIELDS - 1), -(1 << 28), jnp.left_shift(1, shift))
    lane = lax.broadcasted_iota(jnp.int32, (nb.shape[0], width), 1)
    words = jnp.zeros((nb.shape[0], width), jnp.int32)
    for d in range(nb.shape[1]):
        words = words + jnp.where(lane == low[:, d:d + 1], weight[:, d:d + 1], 0)
    words_ref[...] = words
    acc = jnp.zeros(sum_ref.shape, f32)
    for field in range(half):
        acc = acc + dot(expand(words, field), scaled[field * width:(field + 1) * width, :])
    sum_ref[...] = acc


def agg_own(neighbours, embeds, tile=256):
    n, degree = neighbours.shape
    f = embeds.shape[1]
    width = 2 * n // FIELDS
    return call(
        agg_own_body,
        (jax.ShapeDtypeStruct((n, width), jnp.int32), jax.ShapeDtypeStruct((n, f), f32)),
        (n // tile,),
        [pl.BlockSpec((tile, degree), lambda i: (i, 0)), whole((n, f))],
        (pl.BlockSpec((tile, width), lambda i: (i, 0)), pl.BlockSpec((tile, f), lambda i: (i, 0))),
        [pltpu.VMEM((n, f), bf16)],
        flops=2 * n * n * f * 4, nbytes=n * width * 4 + n * f * 8, name="agg_own",
    )(neighbours, embeds)


def nets_body(words_ref, sum_ref, recv_ref, emb_ref, gw_ref, pre_ref, agg_ref, nets_ref, scaled):
    width = words_ref.shape[1]
    half = FIELDS // 2
    f = emb_ref.shape[1]

    @pl.when(pl.program_id(0) == 0)
    def _():
        for field in range(half):
            scaled[field * width:(field + 1) * width, :] = (
                recv_ref[field * width:(field + 1) * width, :].astype(f32)
                * field_scale(field + half)
            ).astype(bf16)

    words = words_ref[...]
    acc = sum_ref[...]
    for field in range(half):
        acc = acc + dot(expand(words, field + half), scaled[field * width:(field + 1) * width, :])
    agg = (acc * 0.125).astype(bf16)
    emb = emb_ref[...]
    pre = dot(emb, gw_ref[:f, :]) + dot(agg, gw_ref[f:, :])
    pre_ref[...] = pre
    agg_ref[...] = agg
    nets_ref[...] = (emb.astype(f32) + gelu_both(pre)[0]).astype(bf16)


def make_nets(words, own_sum, received, embeds, gnn_weight, tile=256):
    n, f = embeds.shape
    width = words.shape[1]
    row = lambda i: (i, 0)
    return call(
        nets_body,
        (
            jax.ShapeDtypeStruct((n, f), f32),
            jax.ShapeDtypeStruct((n, f), bf16),
            jax.ShapeDtypeStruct((n, f), bf16),
        ),
        (n // tile,),
        [
            pl.BlockSpec((tile, width), row), pl.BlockSpec((tile, f), row), whole((n, f)),
            pl.BlockSpec((tile, f), row), whole(gnn_weight.shape),
        ],
        tuple(pl.BlockSpec((tile, f), row) for _ in range(3)),
        [pltpu.VMEM((n, f), bf16)],
        flops=2 * n * n * f * 4, nbytes=n * width * 4 + n * f * 16, name="make_nets",
    )(words, own_sum, received, embeds, gnn_weight)


def column(ids_ref, q):
    return ids_ref[...].T[:, q:q + 1]


def one_hot(ids, n):
    return (ids == lax.broadcasted_iota(jnp.int32, (ids.shape[0], n), 1)).astype(f32).astype(bf16)


def pick(ids_all, q, count):
    lane = lax.broadcasted_iota(jnp.int32, ids_all.shape, 1)
    return jnp.sum(jnp.where(lane == q, ids_all, 0), axis=1, keepdims=True)


def gather_body(ids_ref, table_ref, out_ref):
    ids = ids_ref[0].T
    out_ref[0] = dot(one_hot(ids, table_ref.shape[0]), table_ref[...]).astype(bf16)


def gather_rows(ids, table):
    groups, count = ids.shape
    n, f = table.shape
    return call(
        gather_body,
        jax.ShapeDtypeStruct((groups, count, f), bf16),
        (groups,),
        [pl.BlockSpec((1, 1, count), lambda i: (i, 0, 0)), whole((n, f))],
        pl.BlockSpec((1, count, f), lambda i: (i, 0, 0)),
        flops=2 * groups * count * n * f, nbytes=groups * count * f * 2, name="gather_rows",
    )(ids.reshape(groups, 1, count), table)


def victim_body(ids_ref, table_ref, w_ref, out_ref):
    ids = ids_ref[0].T
    rows = dot(one_hot(ids, table_ref.shape[0]), table_ref[...]).astype(bf16)
    out_ref[0] = dot(rows, w_ref[...])


def victim_part(ids, table, w1a):
    groups, count = ids.shape
    n, f = table.shape
    return call(
        victim_body,
        jax.ShapeDtypeStruct((groups, count, w1a.shape[1]), f32),
        (groups,),
        [pl.BlockSpec((1, 1, count), lambda i: (i, 0, 0)), whole((n, f)), whole(w1a.shape)],
        pl.BlockSpec((1, count, w1a.shape[1]), lambda i: (i, 0, 0)),
        flops=2 * groups * count * (n + f) * f, nbytes=groups * count * f * 4, name="victim_part",
    )(ids.reshape(groups, 1, count), table, w1a)


def pair_body(part_ref, va_ref, w1b_ref, w2m_ref, w2_ref, tgt_ref, cnt_ref, grad_ref, w2g_ref, sq_ref):
    q = pl.program_id(0)
    linear = va_ref[0] + dot(part_ref[0], w1b_ref[...])
    act, slope = gelu_both(linear)
    act = act.astype(bf16)
    scores = dot(act, w2m_ref[...])
    count = scores.shape[0]
    target = tgt_ref[0].T
    live = lax.broadcasted_iota(jnp.int32, (count, 1), 0) < cnt_ref[0, q]
    errors = jnp.where(live, scores - target, 0.0)
    residual = 2.0 * errors
    grad_ref[0] = (residual * w2_ref[...].astype(f32) * slope).astype(bf16)

    @pl.when(q == 0)
    def _():
        w2g_ref[...] = jnp.zeros_like(w2g_ref)
        sq_ref[...] = jnp.zeros_like(sq_ref)

    w2g_ref[...] += jnp.sum(residual * act.astype(f32), axis=0, keepdims=True)
    sq_ref[...] += jnp.sum(errors * errors, axis=0, keepdims=True)


def pair_step(partner, va, w1b, w2, targets, counts):
    groups, count, f = partner.shape
    h = w1b.shape[1]
    block = lambda i: (i, 0, 0)
    return call(
        pair_body,
        (
            jax.ShapeDtypeStruct((groups, count, h), bf16),
            jax.ShapeDtypeStruct((1, h), f32),
            jax.ShapeDtypeStruct((1, h), f32),
        ),
        (groups,),
        [
            pl.BlockSpec((1, count, f), block), pl.BlockSpec((1, count, h), block),
            whole((f, h)), whole((h, h)), whole((1, h)),
            pl.BlockSpec((1, 1, count), block), pl.BlockSpec(memory_space=pltpu.SMEM),
        ],
        (pl.BlockSpec((1, count, h), block), whole((1, h)), whole((1, h))),
        flops=2 * groups * count * 2 * f * h, nbytes=groups * count * h * 8, name="pair_step",
    )(
        partner, va, w1b, jnp.broadcast_to(w2[:, None], (h, h)), w2[None, :],
        targets.reshape(groups, 1, count), counts,
    )


def split(value):
    high = value.astype(bf16)
    return high, (value - high.astype(f32)).astype(bf16)


def scatter_loop(ids_ref, grad_ref, acc, tile):
    groups, count, f = grad_ref.shape
    n = acc.shape[0]

    def step(i, _):
        base = pl.multiple_of(i * tile, tile)
        row = lax.broadcasted_iota(jnp.int32, (tile, count), 0) + base
        total = jnp.zeros((tile, f), f32)
        for q in range(groups):
            hot = (row == ids_ref[q:q + 1, :]).astype(f32).astype(bf16)
            total = total + dot(hot, grad_ref[q])
        acc[pl.ds(base, tile), :] = total
        return 0

    lax.fori_loop(0, n // tile, step, 0)


def scatter_victim_body(ids_ref, grad_ref, nets_ref, w_ref, ng_ref, wg_ref, acc):
    scatter_loop(ids_ref, grad_ref, acc, 256)
    high, low = split(acc[...])
    ng_ref[...] = lax.dot_general(high, w_ref[...], contract_cols, preferred_element_type=f32) + lax.dot_general(low, w_ref[...], contract_cols, preferred_element_type=f32)
    nets = nets_ref[...]
    wg_ref[...] = lax.dot_general(nets, high, contract_rows, preferred_element_type=f32) + lax.dot_general(nets, low, contract_rows, preferred_element_type=f32)


def scatter_victim(ids, grad, nets, w1a):
    n, f = nets.shape
    h = w1a.shape[1]
    groups, count, _ = grad.shape
    return call(
        scatter_victim_body,
        (jax.ShapeDtypeStruct((n, f), f32), jax.ShapeDtypeStruct((f, h), f32)),
        (1,),
        [whole(ids.shape), whole(grad.shape), whole(nets.shape), whole(w1a.shape)],
        (whole((n, f)), whole((f, h))),
        [pltpu.VMEM((n, h), f32)],
        flops=2 * groups * count * n * h, nbytes=groups * count * h * 2 + n * f * 6, name="scatter_victim",
    )(ids, grad, nets, w1a)


def back_body(ids_ref, grad_ref, nets_ref, w_ref, ngv_ref, pre_ref, emb_ref, agg_ref, gw_ref, wg_ref, gg_ref, base_ref, ag_ref, acc):
    scatter_loop(ids_ref, grad_ref, acc, 256)
    f = emb_ref.shape[1]
    tile = 256

    def step(i, _):
        rows = pl.ds(pl.multiple_of(i * tile, tile), tile)
        high, low = split(acc[rows, :])
        w = w_ref[...]
        ng = ngv_ref[rows, :] + lax.dot_general(high, w, contract_cols, preferred_element_type=f32) + lax.dot_general(low, w, contract_cols, preferred_element_type=f32)
        pg = (ng * gelu_slope(pre_ref[rows, :])).astype(bf16)
        cat_own = lax.dot_general(pg, gw_ref[:f, :], contract_cols, preferred_element_type=f32)
        cat_agg = lax.dot_general(pg, gw_ref[f:, :], contract_cols, preferred_element_type=f32)
        base_ref[rows, :] = ng + cat_own
        ag_ref[rows, :] = (cat_agg * 0.125).astype(bf16)
        nets = nets_ref[rows, :]
        wg = lax.dot_general(nets, high, contract_rows, preferred_element_type=f32) + lax.dot_general(nets, low, contract_rows, preferred_element_type=f32)
        g1 = lax.dot_general(emb_ref[rows, :], pg, contract_rows, preferred_element_type=f32)
        g2 = lax.dot_general(agg_ref[rows, :], pg, contract_rows, preferred_element_type=f32)
        wg_ref[...] += wg
        gg_ref[:f, :] += g1
        gg_ref[f:, :] += g2
        return 0

    wg_ref[...] = jnp.zeros_like(wg_ref)
    gg_ref[...] = jnp.zeros_like(gg_ref)
    lax.fori_loop(0, acc.shape[0] // tile, step, 0)


def back(ids, grad, nets, w1b, ngv, pre, embeds, aggregate, gnn_weight):
    n, f = nets.shape
    h = w1b.shape[1]
    groups, count, _ = grad.shape
    args = (ids, grad, nets, w1b, ngv, pre, embeds, aggregate, gnn_weight)
    return call(
        back_body,
        (
            jax.ShapeDtypeStruct((f, h), f32), jax.ShapeDtypeStruct((2 * f, f), f32),
            jax.ShapeDtypeStruct((n, f), f32), jax.ShapeDtypeStruct((n, f), bf16),
        ),
        (1,),
        [whole(a.shape) for a in args],
        (whole((f, h)), whole((2 * f, f)), whole((n, f)), whole((n, f))),
        [pltpu.VMEM((n, h), f32)],
        flops=2 * groups * count * n * h, nbytes=groups * count * h * 2 + n * f * 20, name="back",
    )(*args)


def table_body(first, words_ref, ag_ref, out_ref):
    for j in range(FIELDS // 2):
        hot = expand(words_ref[...], first + j)
        part = lax.dot_general(hot, ag_ref[...], contract_rows, preferred_element_type=f32)
        out_ref[j] = (part * field_scale(first + j)).astype(out_ref.dtype)


def table_back(words, ag, first, dtype, name, tile=256):
    n, width = words.shape
    f = ag.shape[1]
    half = FIELDS // 2
    out = call(
        functools.partial(table_body, first),
        jax.ShapeDtypeStruct((half, width, f), dtype),
        (width // tile,),
        [pl.BlockSpec((n, tile), lambda i: (0, i)), whole((n, f))],
        pl.BlockSpec((half, tile, f), lambda i: (0, i, 0)),
        flops=2 * n * n * f * 2, nbytes=n * width * 4 + n * f * 6, name=name,
    )(words, ag)
    return out.reshape(half * width, f)


def final_body(ids_ref, ret_ref, base_ref, own_ref, scale_ref, out_ref):
    tile, f = out_ref.shape
    peers, halo = ids_ref.shape
    row = lax.broadcasted_iota(jnp.int32, (tile, halo), 0) + pl.program_id(0) * tile
    total = base_ref[...] + own_ref[...]
    for p in range(peers):
        hot = (row == ids_ref[p:p + 1, :]).astype(f32).astype(bf16)
        total = total + dot(hot, ret_ref[p])
    out_ref[...] = (total * scale_ref[0]).astype(bf16)


def final(ids, returned, base, own, scale, tile=256):
    n, f = base.shape
    row = lambda i: (i, 0)
    return call(
        final_body,
        jax.ShapeDtypeStruct((n, f), bf16),
        (n // tile,),
        [
            whole(ids.shape), whole(returned.shape), pl.BlockSpec((tile, f), row),
            pl.BlockSpec((tile, f), row), pl.BlockSpec(memory_space=pltpu.SMEM),
        ],
        pl.BlockSpec((tile, f), row),
        flops=2 * n * n * f, nbytes=n * f * 12, name="final",
    )(ids, returned, base, own, scale)
MESH = pl.DeviceIdType.MESH


def reduce_body(n_chip, n_dom, x_ref, out_ref, r0, s0, r1, s1, r2, s2, e0, ea, e1, eb, e2,
                send0, recv0, send1, recv1, send2, recv2, gsend0, grecv0, gsend1, grecv1, gsend2, grecv2,
                es0, er0, es1, er1, es2, er2):
    region = lax.axis_index("region")
    dom = lax.axis_index("dom")
    core = lax.rem(region, 2)
    chip = region // 2
    rows = out_ref.shape[0] - 8
    q0 = rows // 2
    q1 = q0 // n_chip
    q2 = q1 // n_dom

    def at(r, d):
        return (r, d)

    pair = at(chip * 2 + 1 - core, dom)
    chips = [at(lax.rem(chip + k, n_chip) * 2 + core, dom) for k in range(1, n_chip)]
    doms = [at(region, lax.rem(dom + k, n_dom)) for k in range(1, n_dom)]
    barrier = pltpu.get_barrier_semaphore()
    for device in [pair] + chips + doms:
        pl.semaphore_signal(barrier, inc=1, device_id=device, device_id_type=MESH)
    pl.semaphore_wait(barrier, 1 + len(chips) + len(doms))

    def send(src, dst, ssem, rsem, device):
        copy = pltpu.make_async_remote_copy(src_ref=src, dst_ref=dst, send_sem=ssem, recv_sem=rsem,
                                            device_id=device, device_id_type=MESH)
        copy.start()
        return copy

    c0 = send(x_ref.at[pl.ds((1 - core) * q0, q0)], r0, send0, recv0, pair)
    c0e = send(x_ref.at[pl.ds(rows, 8)], e0, es0, er0, pair)
    c0.wait()
    c0e.wait()
    s0[...] = x_ref[pl.ds(core * q0, q0), :] + r0[...]
    ea[...] = x_ref[pl.ds(rows, 8), :] + e0[...]
    copies = []
    for k in range(1, n_chip):
        peer = lax.rem(chip + k, n_chip)
        copies.append(send(s0.at[pl.ds(peer * q1, q1)], r1.at[k - 1], send1.at[k - 1], recv1.at[k - 1], chips[k - 1]))
        copies.append(send(ea, e1.at[k - 1], es1.at[k - 1], er1.at[k - 1], chips[k - 1]))
    for copy in copies:
        copy.wait()
    total = s0[pl.ds(chip * q1, q1), :]
    etotal = ea[...]
    for k in range(1, n_chip):
        total = total + r1[k - 1]
        etotal = etotal + e1[k - 1]
    s1[...] = total
    eb[...] = etotal
    copies = []
    for k in range(1, n_dom):
        peer = lax.rem(dom + k, n_dom)
        copies.append(send(s1.at[pl.ds(peer * q2, q2)], r2.at[k - 1], send2.at[k - 1], recv2.at[k - 1], doms[k - 1]))
        copies.append(send(eb, e2.at[k - 1], es2.at[k - 1], er2.at[k - 1], doms[k - 1]))
    for copy in copies:
        copy.wait()
    total = s1[pl.ds(dom * q2, q2), :]
    etotal = eb[...]
    for k in range(1, n_dom):
        total = total + r2[k - 1]
        etotal = etotal + e2[k - 1]
    mine = core * q0 + chip * q1 + dom * q2
    out_ref[pl.ds(mine, q2), :] = total
    out_ref[pl.ds(rows, 8), :] = etotal
    block = out_ref.at[pl.ds(mine, q2)]
    copies = [send(block, block, gsend2.at[k - 1], grecv2.at[k - 1], doms[k - 1]) for k in range(1, n_dom)]
    for copy in copies:
        copy.wait()
    block = out_ref.at[pl.ds(core * q0 + chip * q1, q1)]
    copies = [send(block, block, gsend1.at[k - 1], grecv1.at[k - 1], chips[k - 1]) for k in range(1, n_chip)]
    for copy in copies:
        copy.wait()
    block = out_ref.at[pl.ds(core * q0, q0)]
    send(block, block, gsend0, grecv0, pair).wait()


def reduce_all(x, n_region, n_dom):
    rows = x.shape[0] - 8
    f = x.shape[1]
    n_chip = n_region // 2
    q0 = rows // 2
    q1 = q0 // n_chip
    q2 = q1 // n_dom
    dma = pltpu.SemaphoreType.DMA
    vm = lambda *shape: pltpu.VMEM(shape, f32)
    return pl.pallas_call(
        functools.partial(reduce_body, n_chip, n_dom),
        out_shape=jax.ShapeDtypeStruct(x.shape, f32),
        in_specs=[pl.BlockSpec(memory_space=pltpu.VMEM)],
        out_specs=pl.BlockSpec(memory_space=pltpu.VMEM),
        scratch_shapes=[
            vm(q0, f), vm(q0, f), vm(n_chip - 1, q1, f), vm(q1, f), vm(n_dom - 1, q2, f), vm(q2, f),
            vm(8, f), vm(8, f), vm(n_chip - 1, 8, f), vm(8, f), vm(n_dom - 1, 8, f),
            dma, dma, dma((n_chip - 1,)), dma((n_chip - 1,)), dma((n_dom - 1,)), dma((n_dom - 1,)),
            dma, dma, dma((n_chip - 1,)), dma((n_chip - 1,)), dma((n_dom - 1,)), dma((n_dom - 1,)),
            dma, dma, dma((n_chip - 1,)), dma((n_chip - 1,)), dma((n_dom - 1,)), dma((n_dom - 1,)),
        ],
        name="reduce_all",
        compiler_params=pltpu.CompilerParams(collective_id=0, has_side_effects=True, vmem_limit_bytes=VMEM_LIMIT),
    )(x)
def local(
    embeds, neighbours, halo_send, gnn_weight, pair_local, pair_remote, pair_count, targets, pair_w1, pair_w2
):
    n, f = embeds.shape
    peers, halo = halo_send.shape
    regions, slots = pair_local.shape
    n_region, n_dom = lax.axis_size("region"), lax.axis_size("dom")
    nets_total = n * n_region * n_dom
    w1a, w1b = pair_w1[:f], pair_w1[f:]
    exchange = functools.partial(lax.all_to_all, split_axis=0, concat_axis=0, tiled=True)

    outgoing = gather_rows(halo_send.reshape(4, -1), embeds).reshape(peers, halo, f)
    received = exchange(outgoing, "dom").reshape(-1, f)
    asked = exchange(pair_remote, "region")
    words, own_sum = agg_own(neighbours, embeds)
    pre, aggregate, nets = make_nets(words, own_sum, received, embeds, gnn_weight)
    partner = exchange(gather_rows(asked, nets), "region")
    va = victim_part(pair_local, nets, w1a)
    lin_grad, w2_grad, sq = pair_step(partner, va, w1b, pair_w2, targets, pair_count)
    returned = exchange(lin_grad, "region")
    ng_victim, w1a_grad = scatter_victim(pair_local, lin_grad, nets, w1a)
    w1b_grad, gnn_grad, base, agg_grad = back(
        asked, returned, nets, w1b, ng_victim, pre, embeds, aggregate, gnn_weight
    )
    halo_back = table_back(words, agg_grad, FIELDS // 2, bf16, "halo_back").reshape(peers, halo, f)
    returned_halo = exchange(halo_back, "dom")
    own = table_back(words, agg_grad, 0, f32, "own_back")
    extra = jnp.concatenate(
        [
            w2_grad, sq,
            jnp.broadcast_to(jnp.sum(pair_count).astype(f32), (1, f)),
            jnp.zeros((5, f), f32),
        ],
        0,
    )
    sums = reduce_all(jnp.concatenate([gnn_grad, w1a_grad, w1b_grad, extra], 0), n_region, n_dom)
    total = sums[4 * f + 2, 0]
    root = 8.0 / jnp.sqrt(total)
    scale = (8.0 * nets_total / total).reshape(1)
    embeds_grad = final(halo_send, returned_halo, base, own, scale)
    return (
        embeds_grad,
        sums[: 2 * f] * root,
        sums[2 * f : 4 * f] * root,
        sums[4 * f] * root,
        sums[4 * f + 1, 0] / total,
    )


def solution(mesh):
    both = P(("region", "dom"), None)
    in_specs = (both, both, both, P(), both, both, both, both, P(), P())
    out_specs = (both, P(), P(), P(), P())
    return jax.shard_map(local, mesh=mesh, in_specs=in_specs, out_specs=out_specs, check_vma=False)
```

time: 456 us -> 231 us (0.51)
  Pallas kernels: 0 us -> 145 us
  matrix products: 118 us -> 0 us
  waiting for transfers between devices: 104 us -> 32.2 us
  blocking collectives: 68 us -> 0 us
  other arithmetic: 63.1 us -> 2.23 us
  local copies, waits for them, and re-layouts: 49.6 us -> 14.7 us
  between operations: 19.1 us -> 5.25 us
    pallas_call x0 -> x12, Pallas kernels: none -> 145 us  [the longest x1 37.2 us: reduce_all(): pl.pallas_call(functools.partial(reduce_body, n_chip, n_dom), out_shape=j...]
    dot_general x11 -> x0, matrix products: 118 us -> none  [the longest x1 50 us: local(): agg_sum = jnp.dot(adjacency, table, preferred_element_type=jnp.float32)]
    psum x1 -> x0, waiting for transfers between devices: 80.3 us -> none  [local(): lax.psum((grad_gnn, grad_w1, grad_w2, sq_local), ('region', 'dom'))]
    psum x1 -> x0, blocking collectives: 68 us -> none  [local(): total_count = lax.psum(local_count, ('region', 'dom'))]
    scatter-add x2 -> x0, other arithmetic: 50.8 us -> none  [the longest x1 26.2 us: local(): nets_grad.at[asked.reshape(-1)]]
    gather x2 -> x0, local copies, waits for them, and re-layouts: 34 us -> none  [the longest x1 17 us: local(): victim = nets[pair_local]]
    all_to_all x5, waiting for transfers between devices: 23.2 us -> 32.2 us  [the longest x1 14 us: local(): returned = exchange(lin_grad, 'region')]
    unnamed x45 -> x36, local copies, waits for them, and re-layouts: 10.6 us -> 5.35 us
  transfers between devices with their start and end apart: 6 -> 5, of which waited for: 3 -> 4; matrix products, arithmetic and copies ran while one was open for 13% -> 3% of each run, Pallas kernels for 0% -> 22%
where the time goes in v1:
time: 231 us; the launch traced here: 229 us
  Pallas kernels  145 us (63%)
  waiting for transfers between devices  32.2 us (14%)
  starting transfers between devices  29.7 us (13%)
  local copies, waits for them, and re-layouts  14.7 us (6%)
  between operations  5.25 us (2%)
    pallas_call x1, Pallas kernels, reduce_all(): pl.pallas_call(functools.partial(reduce_body, n_chip, n_dom), out_shape=j...  37.2 us
    pallas_call x1, Pallas kernels, back(): call(back_body, (jax.ShapeDtypeStruct((f, h), f32), jax.ShapeDtypeStruct(...  16.8 us
    pallas_call x2, Pallas kernels, gather_rows(): call(gather_body, jax.ShapeDtypeStruct((groups, count, f), bf16), (groups...  15.6 us
    all_to_all x1, waiting for transfers between devices, local(): returned = exchange(lin_grad, 'region')  14 us
    pallas_call x1, Pallas kernels, agg_own(): call(agg_own_body, (jax.ShapeDtypeStruct((n, width), jnp.int32), jax.Shap...  12.6 us
    pallas_call x1, Pallas kernels, victim_part(): call(victim_body, jax.ShapeDtypeStruct((groups, count, w1a.shape[1]), f32...  12.4 us
    all_to_all x1, waiting for transfers between devices, local(): partner = exchange(gather_rows(asked, nets), 'region')  11.3 us
    pallas_call x2, Pallas kernels, table_back(): call(functools.partial(table_body, first), jax.ShapeDtypeStruct((half, wi...  10.8 us
  transfers between devices with their start and end apart: 5, of which 4 were waited for; matrix products, arithmetic and copies ran while one was open for 3% of the time, Pallas kernels for 22%

profile of v1, /device:TPU:1, one launch (start us, length us, event | category | flops | bytes accessed | tf_op | source)
XLA Modules:
  0.0 228.6 jit_solution(8673403927273719547)
XLA Ops:
  0.6 5.8 %gather_rows.2 = bf16[4,512,256]{2,1,0:T(8,128)(2,1)} custom-call(s32[4,1,512]{2,1,0:T(1,128)} %bitcast.17, bf16[2048,256]{1,0:T(8,128)(2,1)} %emb_ref.3), custom_call_target="tpu_custom_call" | custom-call | flops 2147483648 | bytes 1048576 | tf_op jit(solution)/shard_map/gather_rows/pallas_call | solution.py:178
  6.5 8.7 %all-to-all-start.1 = ((bf16[16,128,256]{2,1,0:T(8,128)(2,1)}), bf16[16,128,256]{2,1,0:T(8,128)(2,1)S(1)}, u32[]{:S(2)}, u32[]{:S(2)}) async-start(bf16[16,128,256]{2,1,0:T(8,128)(2,1)} %bitcast.14), calls=%async_computation.1 | async-start | bytes 2097152 | tf_op jit(solution)/shard_map/all_to_all | solution.py:509
  15.2 1.3 copy.17.nb_ref
  17.1 12.6 %agg_own.1 = (s32[2048,512]{1,0:T(8,128)}, f32[2048,256]{1,0:T(8,128)}) custom-call(s32[2048,8]{1,0:T(8,128)} %copy.17.nb_ref, bf16[2048,256]{1,0:T(8,128)(2,1)} %emb_ref.3), custom_call_target="tpu_custom_call" | custom-call | flops 8589934592 | bytes 8388608 | tf_op jit(solution)/shard_map/agg_own/pallas_call | solution.py:99
  29.7 1.1 all-to-all-done.1
  30.9 7.3 %all-to-all-start = ((s32[8,1,512]{2,1,0:T(1,128)}), s32[8,1,512]{2,1,0:T(1,128)S(1)}, u32[]{:S(2)}, u32[]{:S(2)}) async-start(s32[8,1,512]{2,1,0:T(1,128)} %all_to_all.19), calls=%async_computation | async-start | bytes 32768 | tf_op jit(solution)/shard_map/all_to_all | solution.py:510
  38.2 10.5 %make_nets.1 = (f32[2048,256]{1,0:T(8,128)}, bf16[2048,256]{1,0:T(8,128)(2,1)}, bf16[2048,256]{1,0:T(8,128)(2,1)}) custom-call(s32[2048,512]{1,0:T(8,128)} %get-tuple-element.19.words_ref, f32[2048,256]{1,0:T(8,128)} %get-tuple-element.20.sum_ref, bf16[2048,256]{1,0:T(8,128)(2,1)} %bitcast.13, bf16[2048,256]{1,0:T(8,128)(2,1)} %emb_ref.3, ...), custom_call_target="tpu_custom_call" | custom-call | flops 8589934592 | bytes 12582912 | tf_op jit(solution)/shard_map/make_nets/pallas_call | solution.py:139
  49.3 9.8 %gather_rows.3 = bf16[8,512,256]{2,1,0:T(8,128)(2,1)} custom-call(s32[8,1,512]{2,1,0:T(1,128)} %copy-done.8, bf16[2048,256]{1,0:T(8,128)(2,1)} %get-tuple-element.21.table_ref.nets_ref), custom_call_target="tpu_custom_call" | custom-call | flops 4294967296 | bytes 2097152 | tf_op jit(solution)/shard_map/gather_rows/pallas_call | solution.py:178
  59.1 4.9 %all-to-all-start.2 = ((bf16[8,512,256]{2,1,0:T(8,128)(2,1)}), bf16[8,512,256]{2,1,0:T(8,128)(2,1)S(1)}, u32[]{:S(2)}, u32[]{:S(2)}) async-start(bf16[8,512,256]{2,1,0:T(8,128)(2,1)} %gather_rows.3), calls=%async_computation.2 | async-start | bytes 4194304 | tf_op jit(solution)/shard_map/all_to_all | solution.py:513
  66.6 12.4 %victim_part.1.va_ref = f32[8,512,256]{2,1,0:T(8,128)} custom-call(s32[8,1,512]{2,1,0:T(1,128)} %reshape.44.ids_ref, bf16[2048,256]{1,0:T(8,128)(2,1)} %get-tuple-element.21.table_ref.nets_ref, bf16[256,256]{1,0:T(8,128)(2,1)} %get-tuple-element.38.w_ref), custom_call_target="tpu_custom_call" | custom-call | flops 4831838208 | bytes 4194304 | tf_op jit(solution)/shard_map/victim_part/pallas_call | solution.py:197
  79.0 11.3 %all-to-all-done.2.part_ref = bf16[8,512,256]{2,1,0:T(8,128)(2,1)S(1)} async-done(((bf16[8,512,256]{2,1,0:T(8,128)(2,1)}), bf16[8,512,256]{2,1,0:T(8,128)(2,1)S(1)}, u32[]{:S(2)}, u32[]{:S(2)}) %all-to-all-start.2) | async-done | bytes 2097184 | tf_op jit(solution)/shard_map/all_to_all | solution.py:513
  91.6 9.3 %pair_step.1 = (bf16[8,512,256]{2,1,0:T(8,128)(2,1)}, f32[1,256]{1,0:T(1,128)}, f32[1,256]{1,0:T(1,128)}) custom-call(bf16[8,512,256]{2,1,0:T(8,128)(2,1)} %copy-done, f32[8,512,256]{2,1,0:T(8,128)} %victim_part.1.va_ref, bf16[256,256]{1,0:T(8,128)(2,1)} %get-tuple-element.37.w1b_ref.w_ref, bf16[256,256]{1,0:T(8,128)(2,1)} %broadcast_in_dim.15.w2m_ref, ...), custom_call_target="tpu_custom_call" | custom-call | flops 1073741824 | bytes 8388608 | tf_op jit(solution)/shard_map/pair_step/pallas_call | solution.py:233
  101.0 4.6 %all-to-all-start.3 = ((bf16[8,512,256]{2,1,0:T(8,128)(2,1)}), bf16[8,512,256]{2,1,0:T(8,128)(2,1)S(1)}, u32[]{:S(2)}, u32[]{:S(2)}) async-start(bf16[8,512,256]{2,1,0:T(8,128)(2,1)} %get-tuple-element.22.grad_ref), calls=%async_computation.3 | async-start | bytes 4194304 | tf_op jit(solution)/shard_map/all_to_all | solution.py:516
  107.5 10.3 %scatter_victim.1 = (f32[2048,256]{1,0:T(8,128)}, f32[256,256]{1,0:T(8,128)}) custom-call(s32[8,512]{1,0:T(8,128)} %ids_ref.2, bf16[8,512,256]{2,1,0:T(8,128)(2,1)} %get-tuple-element.22.grad_ref, bf16[2048,256]{1,0:T(8,128)(2,1)} %get-tuple-element.21.table_ref.nets_ref, bf16[256,256]{1,0:T(8,128)(2,1)} %get-tuple-element.38.w_ref), custom_call_target="tpu_custom_call" | custom-call | flops 4294967296 | bytes 5242880 | tf_op jit(solution)/shard_map/scatter_victim/pallas_call | solution.py:288
  117.8 14.0 %all-to-all-done.3.grad_ref = bf16[8,512,256]{2,1,0:T(8,128)(2,1)S(1)} async-done(((bf16[8,512,256]{2,1,0:T(8,128)(2,1)}), bf16[8,512,256]{2,1,0:T(8,128)(2,1)S(1)}, u32[]{:S(2)}, u32[]{:S(2)}) %all-to-all-start.3) | async-done | bytes 2097184 | tf_op jit(solution)/shard_map/all_to_all | solution.py:516
  131.8 1.4 copy-done.2
  133.2 16.8 %back.1 = (f32[256,256]{1,0:T(8,128)}, f32[512,256]{1,0:T(8,128)}, f32[2048,256]{1,0:T(8,128)}, bf16[2048,256]{1,0:T(8,128)(2,1)}) custom-call(s32[8,512]{1,0:T(8,128)} %bitcast.15, bf16[8,512,256]{2,1,0:T(8,128)(2,1)} %copy-done.2, bf16[2048,256]{1,0:T(8,128)(2,1)} %get-tuple-element.21.table_ref.nets_ref, ...), custom_call_target="tpu_custom_call" | custom-call | flops 4294967296 | bytes 12582912 | tf_op jit(solution)/shard_map/back/pallas_call | solution.py:333
  150.0 4.8 %concatenate.3.x_ref = f32[1032,256]{1,0:T(8,128)} concatenate(f32[512,256]{1,0:T(8,128)} %get-tuple-element.28, f32[256,256]{1,0:T(8,128)S(1)} %copy-done.5, f32[256,256]{1,0:T(8,128)} %get-tuple-element.30, f32[1,256]{1,0:T(1,128)S(1)} %copy-done.13, f32[1,256]{1,0:T(1,128)S(1)} %copy-done.14, f32[1,256]{1,0:T(1,128)S(1)} %broadcast_in_dim.17, f32[5,256]{1,0:T(8,128)S(1)} %broadcast_in_dim.18), dimensions={0} | concatenate | bytes 2113536 | tf_op jit(solution)/shard_map/concatenate | solution.py:532
  154.8 37.2 %reduce_all.1 = f32[1032,256]{1,0:T(8,128)} custom-call(f32[1032,256]{1,0:T(8,128)} %concatenate.3.x_ref), custom_call_target="tpu_custom_call" | custom-call | tf_op jit(solution)/shard_map/reduce_all/pallas_call | solution.py:482
  192.0 5.3 %halo_back.1 = bf16[4,512,256]{2,1,0:T(8,128)(2,1)} custom-call(s32[2048,512]{1,0:T(8,128)} %get-tuple-element.19.words_ref, bf16[2048,256]{1,0:T(8,128)(2,1)} %get-tuple-element.26.ag_ref), custom_call_target="tpu_custom_call" | custom-call | flops 4294967296 | bytes 7340032 | tf_op jit(solution)/shard_map/halo_back/pallas_call | solution.py:358
  197.3 4.1 %all-to-all-start.4 = ((bf16[16,128,256]{2,1,0:T(8,128)(2,1)}), bf16[16,128,256]{2,1,0:T(8,128)(2,1)S(1)}, u32[]{:S(2)}, u32[]{:S(2)}) async-start(bf16[16,128,256]{2,1,0:T(8,128)(2,1)} %bitcast.12), calls=%async_computation.4 | async-start | bytes 2097152 | tf_op jit(solution)/shard_map/all_to_all | solution.py:522
  206.3 5.5 %own_back.1 = f32[4,512,256]{2,1,0:T(8,128)} custom-call(s32[2048,512]{1,0:T(8,128)} %get-tuple-element.19.words_ref, bf16[2048,256]{1,0:T(8,128)(2,1)} %get-tuple-element.26.ag_ref), custom_call_target="tpu_custom_call" | custom-call | flops 4294967296 | bytes 7340032 | tf_op jit(solution)/shard_map/own_back/pallas_call | solution.py:358
  211.8 5.7 %all-to-all-done.4.ret_ref = bf16[16,128,256]{2,1,0:T(8,128)(2,1)S(1)} async-done(((bf16[16,128,256]{2,1,0:T(8,128)(2,1)}), bf16[16,128,256]{2,1,0:T(8,128)(2,1)S(1)}, u32[]{:S(2)}, u32[]{:S(2)}) %all-to-all-start.4) | async-done | bytes 1048608 | tf_op jit(solution)/shard_map/all_to_all | solution.py:522
  218.5 8.9 %final.1 = bf16[2048,256]{1,0:T(8,128)(2,1)} custom-call(s32[16,128]{1,0:T(8,128)} %ids_ref.3, bf16[16,128,256]{2,1,0:T(8,128)(2,1)} %copy-done.3, f32[2048,256]{1,0:T(8,128)} %get-tuple-element.27.base_ref, f32[2048,256]{1,0:T(8,128)} %bitcast.18, f32[1]{0:T(128)} %bitcast.5.scale_ref), custom_call_target="tpu_custom_call" | custom-call | flops 2147483648 | bytes 6291456 | tf_op jit(solution)/shard_map/final/pallas_call | solution.py:383
  (47 shorter events, 9.5 us)
Async XLA Ops:
  6.5 8.7 %copy-start.7 = (s32[2048,8]{0,1:T(8,128)S(1)}, s32[2048,8]{0,1:T(8,128)}, u32[]{:S(2)}) copy-start(s32[2048,8]{0,1:T(8,128)} %param.11) | copy-start | bytes 196612
  6.5 10.1 %copy-start.10 = (s32[8,512]{1,0:T(8,128)S(1)}, s32[8,512]{1,0:T(8,128)}, u32[]{:S(2)}) copy-start(s32[8,512]{1,0:T(8,128)} %param.15) | copy-start | bytes 49156
  6.5 24.4 %all-to-all-start.1 = ((bf16[16,128,256]{2,1,0:T(8,128)(2,1)}), bf16[16,128,256]{2,1,0:T(8,128)(2,1)S(1)}, u32[]{:S(2)}, u32[]{:S(2)}) async-start(bf16[16,128,256]{2,1,0:T(8,128)(2,1)} %bitcast.14), calls=%async_computation.1 | async-start | bytes 2097152 | tf_op jit(solution)/shard_map/all_to_all | solution.py:509
  30.9 7.3 %copy-start.4 = (bf16[16,128,256]{2,1,0:T(8,128)(2,1)}, bf16[16,128,256]{2,1,0:T(8,128)(2,1)S(1)}, u32[]{:S(2)}) copy-start(bf16[16,128,256]{2,1,0:T(8,128)(2,1)S(1)} %all-to-all-done.1) | copy-start | bytes 3145732
  30.9 17.8 %all-to-all-start = ((s32[8,1,512]{2,1,0:T(1,128)}), s32[8,1,512]{2,1,0:T(1,128)S(1)}, u32[]{:S(2)}, u32[]{:S(2)}) async-start(s32[8,1,512]{2,1,0:T(1,128)} %all_to_all.19), calls=%async_computation | async-start | bytes 32768 | tf_op jit(solution)/shard_map/all_to_all | solution.py:510
  48.7 0.6 copy-start.8
  59.1 5.0 %copy-start.12 = (s32[8,512]{1,0:T(8,128)S(1)}, s32[8,512]{1,0:T(8,128)}, u32[]{:S(2)}) copy-start(s32[8,512]{1,0:T(8,128)} %ids_ref.2) | copy-start | bytes 49156
  59.1 5.6 %copy-start.11 = (f32[8,512]{1,0:T(8,128)S(1)}, f32[8,512]{1,0:T(8,128)}, u32[]{:S(2)}) copy-start(f32[8,512]{1,0:T(8,128)} %param.17) | copy-start | bytes 49156
  59.1 6.2 %copy-start.15 = (bf16[256]{0:T(256)(128)(2,1)S(1)}, bf16[256]{0:T(256)(128)(2,1)}, u32[]{:S(2)}) copy-start(bf16[256]{0:T(256)(128)(2,1)} %param.19) | copy-start | bytes 1540
  59.1 6.8 %copy-start.6 = (bf16[512,256]{1,0:T(8,128)(2,1)S(1)}, bf16[512,256]{1,0:T(8,128)(2,1)}, u32[]{:S(2)}) copy-start(bf16[512,256]{1,0:T(8,128)(2,1)} %param.18) | copy-start | bytes 786436
  59.1 31.2 %all-to-all-start.2 = ((bf16[8,512,256]{2,1,0:T(8,128)(2,1)}), bf16[8,512,256]{2,1,0:T(8,128)(2,1)S(1)}, u32[]{:S(2)}, u32[]{:S(2)}) async-start(bf16[8,512,256]{2,1,0:T(8,128)(2,1)} %gather_rows.3), calls=%async_computation.2 | async-start | bytes 4194304 | tf_op jit(solution)/shard_map/all_to_all | solution.py:513
  90.3 1.3 copy-start
  101.0 4.6 %copy-start.16 = (s32[1,8]{1,0:T(1,128)S(1)}, s32[1,8]{1,0:T(1,128)}, u32[]{:S(2)}) copy-start(s32[1,8]{1,0:T(1,128)} %cnt_ref.1) | copy-start | bytes 100
  101.0 5.9 %copy-start.9 = (s32[8,1,512]{2,1,0:T(1,128)S(1)}, s32[8,1,512]{2,1,0:T(1,128)}, u32[]{:S(2)}) copy-start(s32[8,1,512]{2,1,0:T(1,128)} %copy-done.8) | copy-start | bytes 49156
  101.0 30.9 %all-to-all-start.3 = ((bf16[8,512,256]{2,1,0:T(8,128)(2,1)}), bf16[8,512,256]{2,1,0:T(8,128)(2,1)S(1)}, u32[]{:S(2)}, u32[]{:S(2)}) async-start(bf16[8,512,256]{2,1,0:T(8,128)(2,1)} %get-tuple-element.22.grad_ref), calls=%async_computation.3 | async-start | bytes 4194304 | tf_op jit(solution)/shard_map/all_to_all | solution.py:516
  131.8 1.4 copy-start.2
  133.2 16.8 %copy-start.5 = (f32[256,256]{1,0:T(8,128)S(1)}, f32[256,256]{1,0:T(8,128)}, u32[]{:S(2)}) copy-start(f32[256,256]{1,0:T(8,128)} %get-tuple-element.29) | copy-start | bytes 786436
  133.2 16.8 %copy-start.13 = (f32[1,256]{1,0:T(1,128)S(1)}, f32[1,256]{1,0:T(1,128)}, u32[]{:S(2)}) copy-start(f32[1,256]{1,0:T(1,128)} %get-tuple-element.31) | copy-start | bytes 3076
  133.2 16.8 %copy-start.14 = (f32[1,256]{1,0:T(1,128)S(1)}, f32[1,256]{1,0:T(1,128)}, u32[]{:S(2)}) copy-start(f32[1,256]{1,0:T(1,128)} %get-tuple-element.32) | copy-start | bytes 3076
  197.3 4.1 %copy-start.1 = (f32[1032,256]{1,0:T(8,128)S(1)}, f32[1032,256]{1,0:T(8,128)}, u32[]{:S(2)}) copy-start(f32[1032,256]{1,0:T(8,128)} %reduce_all.1) | copy-start | bytes 3170308
  197.3 20.2 %all-to-all-start.4 = ((bf16[16,128,256]{2,1,0:T(8,128)(2,1)}), bf16[16,128,256]{2,1,0:T(8,128)(2,1)S(1)}, u32[]{:S(2)}, u32[]{:S(2)}) async-start(bf16[16,128,256]{2,1,0:T(8,128)(2,1)} %bitcast.12), calls=%async_computation.4 | async-start | bytes 2097152 | tf_op jit(solution)/shard_map/all_to_all | solution.py:522
  217.5 1.0 copy-start.3

commit v2 on v0

v2 whole, which is shorter than its diff:
```python
import functools
import jax
import jax.numpy as jnp
from jax import lax
from jax.experimental import pallas as pl
from jax.experimental.pallas import tpu as pltpu
from jax.sharding import PartitionSpec as P

f32 = jnp.float32
bf16 = jnp.bfloat16
gelu_coef = 0.7978845608
contract_rows = (((0,), (0,)), ((), ()))
contract_cols = (((1,), (1,)), ((), ()))
VMEM_LIMIT = 62 * 1024 * 1024
MESH = pl.DeviceIdType.MESH
FIELDS = 8
HALF = FIELDS // 2


def gelu_both(value):
    inner = jnp.tanh(gelu_coef * (value + 0.044715 * value * value * value))
    half = 0.5 * (1.0 + inner)
    slope = half + 0.5 * value * (1.0 - inner * inner) * gelu_coef * (
        1.0 + 3.0 * 0.044715 * value * value
    )
    return value * half, slope


def dot(a, b):
    return jnp.dot(a, b, preferred_element_type=f32)


def dot_rows(a, b):
    return lax.dot_general(a, b, contract_rows, preferred_element_type=f32)


def dot_cols(a, b):
    return lax.dot_general(a, b, contract_cols, preferred_element_type=f32)


def split(value):
    high = value.astype(bf16)
    return high, (value - high.astype(f32)).astype(bf16)


def rows_at(i, tile):
    return pl.ds(pl.multiple_of(i * tile, tile), tile)


def lane_hot(ids, n):
    return (ids == lax.broadcasted_iota(jnp.int32, (ids.shape[0], n), 1)).astype(f32).astype(bf16)


def row_hot(base, tile, ids):
    row = lax.broadcasted_iota(jnp.int32, (tile, ids.shape[1]), 0)
    return (row == ids - base).astype(f32).astype(bf16)


def counts_of(words, field):
    return ((words >> (4 * field)) & 15).astype(f32).astype(bf16)


class Place:
    def __init__(self, n_region, n_dom):
        self.n_region, self.n_dom = n_region, n_dom
        self.n_chip = n_region // 2
        self.per = n_dom // HALF
        self.region = lax.axis_index("region")
        self.dom = lax.axis_index("dom")
        self.chip = self.region // 2
        self.core = lax.rem(self.region, 2)

    def region_to(self, m):
        chip = lax.rem(self.chip + lax.rem(m, self.n_chip), self.n_chip)
        return chip * 2 + lax.rem(self.core + m // self.n_chip, 2)

    def region_from(self, m):
        chip = lax.rem(self.chip + self.n_chip - lax.rem(m, self.n_chip), self.n_chip)
        return chip * 2 + lax.rem(self.core + m // self.n_chip, 2)

    def field_to(self, i):
        return lax.rem(self.dom // self.per + i, HALF)

    def sub_to(self, j):
        return lax.rem(lax.rem(self.dom, self.per) + j, self.per)

    def dom_to(self, k):
        return lax.rem(self.dom + k, self.n_dom)

    def at_region(self, r):
        return (r, self.dom)

    def at_dom(self, d):
        return (self.region, d)


def remote(src, dst, ssem, rsem, device):
    return pltpu.make_async_remote_copy(
        src_ref=src, dst_ref=dst, send_sem=ssem, recv_sem=rsem, device_id=device, device_id_type=MESH
    )


def greet(devices):
    barrier = pltpu.get_barrier_semaphore()
    for device in devices:
        pl.semaphore_signal(barrier, inc=1, device_id=device, device_id_type=MESH)
    pl.semaphore_wait(barrier, len(devices))


def vmem():
    return pl.BlockSpec(memory_space=pltpu.VMEM)


def smem():
    return pl.BlockSpec(memory_space=pltpu.SMEM)


def kernel_call(body, outs, in_specs, scratch, collective, name, out_specs=None):
    single = not isinstance(outs, tuple)
    specs = vmem() if single else tuple(vmem() for _ in outs)
    params = dict(vmem_limit_bytes=VMEM_LIMIT)
    if collective is not None:
        params.update(collective_id=collective, has_side_effects=True)
    return pl.pallas_call(
        body, out_shape=outs, in_specs=in_specs, out_specs=specs, scratch_shapes=scratch, name=name,
        compiler_params=pltpu.CompilerParams(**params),
    )


def head_body(n_region, n_dom, emb, nb, hs, pr, gw, words, pre, agg, nets, asked,
              outgoing, recv, sums, hsend, hrecv, asend, arecv):
    place = Place(n_region, n_dom)
    per = place.per
    n, f = emb.shape
    halo = hs.shape[1]
    greet([place.at_dom(place.dom_to(k)) for k in range(1, n_dom)]
          + [place.at_region(place.region_to(m)) for m in range(1, n_region)])

    def ask(m):
        r = place.region_to(m)
        return remote(pr.at[pl.ds(r, 1)], asked.at[pl.ds(place.region, 1)],
                      asend.at[m], arecv.at[m], place.at_region(r))

    def halo_copy(i, j):
        field, sub = place.field_to(i), place.sub_to(j)
        return remote(outgoing.at[field * per + sub], recv.at[place.dom],
                      hsend.at[i * per + j], hrecv.at[i * per + j], place.at_dom(field * per + sub))

    for m in range(1, n_region):
        ask(m).start()
    asked[pl.ds(place.region, 1), :] = pr[pl.ds(place.region, 1), :]

    for i in range(HALF):
        field = place.field_to(i)
        ids = jnp.concatenate([hs[pl.ds(field * per + s, 1), :] for s in range(per)], 1).T
        rows = dot(lane_hot(ids, n), emb[...]).astype(bf16)
        for s in range(per):
            outgoing[field * per + s] = rows[s * halo:(s + 1) * halo]
        for j in range(per):
            if i or j:
                halo_copy(i, j).start()
    recv[place.dom] = outgoing[place.dom]

    tile = 256
    width = words.shape[1]
    wbits = width.bit_length() - 1

    def own_step(t, _):
        rows = rows_at(t, tile)
        ids = nb[:, rows].T
        low = ids & (width - 1)
        weight = jnp.left_shift(1, 4 * (ids >> wbits))
        lane = lax.broadcasted_iota(jnp.int32, (tile, width), 1)
        word = jnp.zeros((tile, width), jnp.int32)
        for d in range(ids.shape[1]):
            word = word + jnp.where(lane == low[:, d:d + 1], weight[:, d:d + 1], 0)
        words[rows, :] = word
        acc = jnp.zeros((tile, f), f32)
        for field in range(HALF):
            acc = acc + dot(counts_of(word, field), emb[field * width:(field + 1) * width, :])
        sums[rows, :] = acc
        return 0

    lax.fori_loop(0, n // tile, own_step, 0)
    for i in range(HALF):
        for j in range(per):
            if i or j:
                halo_copy(i, j).wait()

    def halo_step(t, _):
        rows = rows_at(t, tile)
        word = words[rows, :]
        acc = sums[rows, :]
        for field in range(HALF):
            table = recv[field * per:(field + 1) * per].reshape(width, f)
            acc = acc + dot(counts_of(word, field + HALF), table)
        mean = (acc * 0.125).astype(bf16)
        own = emb[rows, :]
        lin = dot(own, gw[:f, :]) + dot(mean, gw[f:, :])
        pre[rows, :] = lin
        agg[rows, :] = mean
        nets[rows, :] = (own.astype(f32) + gelu_both(lin)[0]).astype(bf16)
        return 0

    lax.fori_loop(0, n // tile, halo_step, 0)
    for m in range(1, n_region):
        ask(m).wait()


def head(n_region, n_dom, embeds, neighbours, halo_send, pair_remote, gnn_weight):
    n, f = embeds.shape
    peers, halo = halo_send.shape
    width = 2 * n // FIELDS
    dma = pltpu.SemaphoreType.DMA
    shape = jax.ShapeDtypeStruct
    return kernel_call(
        functools.partial(head_body, n_region, n_dom),
        (
            shape((n, width), jnp.int32), shape((n, f), f32), shape((n, f), bf16), shape((n, f), bf16),
            shape(pair_remote.shape, jnp.int32),
        ),
        [vmem()] * 5,
        [
            pltpu.VMEM((peers, halo, f), bf16), pltpu.VMEM((peers, halo, f), bf16), pltpu.VMEM((n, f), f32),
            dma((n_dom,)), dma((n_dom,)), dma((n_region,)), dma((n_region,)),
        ],
        1, "head",
    )(embeds, neighbours.T, halo_send, pair_remote, gnn_weight)


def pair_body(n_region, n_dom, nets, asked, loc, tgt, cnt, w1, w2, sv, sp, small,
              outgoing, partner, grad, back, va, fsend, frecv, bsend, brecv):
    place = Place(n_region, n_dom)
    me = place.region
    n, f = nets.shape
    count = loc.shape[1]
    h = w1.shape[1]
    greet([place.at_region(place.region_to(m)) for m in range(1, n_region)])

    def out_copy(m):
        r = place.region_to(m)
        return remote(outgoing.at[r], partner.at[me], fsend.at[m], frecv.at[m], place.at_region(r))

    def back_copy(m):
        r = place.region_from(m)
        return remote(grad.at[r], back.at[me], bsend.at[m], brecv.at[m], place.at_region(r))

    def fetch(ids_ref, r):
        ids = ids_ref[pl.ds(r, 1), :].T
        return dot(lane_hot(ids, n), nets[...]).astype(bf16)

    def gather_step(m, _):
        outgoing[place.region_to(m)] = fetch(asked, place.region_to(m))
        out_copy(m).start()
        return 0

    lax.fori_loop(1, n_region, gather_step, 0)
    partner[me] = fetch(asked, me)

    def victim_step(q, _):
        va[q] = dot(fetch(loc, q), w1[:f, :])
        return 0

    lax.fori_loop(0, n_region, victim_step, 0)
    w2row = w2[...]
    w2mat = jnp.broadcast_to(w2row.astype(f32), (h, h)).T.astype(bf16)
    w2f = w2row.astype(f32)

    def pair_step(m):
        q = place.region_from(m)
        linear = va[q] + dot(partner[q], w1[f:, :])
        act, slope = gelu_both(linear)
        act = act.astype(bf16)
        scores = dot(act, w2mat)
        target = tgt[pl.ds(q, 1), :].T
        live = lax.broadcasted_iota(jnp.int32, (count, 1), 0) < cnt[0, q]
        errors = jnp.where(live, scores - target, 0.0)
        residual = 2.0 * errors
        grad[q] = (residual * w2f * slope).astype(bf16)
        small[0:1, :] += jnp.sum(residual * act.astype(f32), axis=0, keepdims=True)
        small[1:2, :] += jnp.sum(errors * errors, axis=0, keepdims=True)

    small[...] = jnp.zeros_like(small)
    live_count = cnt[0, 0]
    for q in range(1, n_region):
        live_count = live_count + cnt[0, q]
    small[2:3, :] = jnp.zeros((1, h), f32) + live_count.astype(f32)
    pair_step(0)

    def away_step(m, _):
        out_copy(m).wait_recv()
        pair_step(m)
        back_copy(m).start()
        return 0

    lax.fori_loop(1, n_region, away_step, 0)
    tile = 512

    def victim_scatter(t, _):
        total = jnp.zeros((tile, h), f32)
        for q in range(n_region):
            total = total + dot(row_hot(t * tile, tile, loc[q:q + 1, :]), grad[q])
        sv[rows_at(t, tile), :] = total
        return 0

    lax.fori_loop(0, n // tile, victim_scatter, 0)

    def self_scatter(t, _):
        sp[rows_at(t, tile), :] = dot(row_hot(t * tile, tile, asked[pl.ds(me, 1), :]), grad[me])
        return 0

    lax.fori_loop(0, n // tile, self_scatter, 0)

    def partner_scatter(m, _):
        r = place.region_to(m)
        back_copy(m).wait_recv()
        ids = asked[pl.ds(r, 1), :]
        rows_back = back[r]
        for t in range(n // tile):
            sp[t * tile:(t + 1) * tile, :] += dot(row_hot(t * tile, tile, ids), rows_back)
        return 0

    lax.fori_loop(1, n_region, partner_scatter, 0)

    def drain(m, _):
        out_copy(m).wait_send()
        back_copy(m).wait_send()
        return 0

    lax.fori_loop(1, n_region, drain, 0)


def pair(n_region, n_dom, nets, asked, pair_local, targets, pair_count, pair_w1, pair_w2):
    n, f = nets.shape
    h = pair_w1.shape[1]
    regions, slots = pair_local.shape
    dma = pltpu.SemaphoreType.DMA
    shape = jax.ShapeDtypeStruct
    blocks = pltpu.VMEM((regions, slots, f), bf16)
    return kernel_call(
        functools.partial(pair_body, n_region, n_dom),
        (shape((n, h), f32), shape((n, h), f32), shape((8, h), f32)),
        [vmem()] * 4 + [smem()] + [vmem()] * 2,
        [blocks, blocks, blocks, blocks, pltpu.VMEM((regions, slots, h), f32)] + [dma((n_region,))] * 4,
        2, "pair",
    )(nets, asked, pair_local, targets, pair_count, pair_w1, pair_w2[None, :])


def middle_body(sv, sp, nets, pre, emb, agg, w1, gw, small, base, ag, load):
    n, f = nets.shape
    tile = 256

    load[:4 * f, :] = jnp.zeros((4 * f, f), f32)
    load[4 * f:, :] = small[...]

    def step(t, _):
        rows = rows_at(t, tile)
        vh, vl = split(sv[rows, :])
        ph, plo = split(sp[rows, :])
        ng = dot_cols(vh, w1[:f, :]) + dot_cols(vl, w1[:f, :]) + dot_cols(ph, w1[f:, :]) + dot_cols(plo, w1[f:, :])
        pg = (ng * gelu_both(pre[rows, :])[1]).astype(bf16)
        base[rows, :] = ng + dot_cols(pg, gw[:f, :])
        ag[rows, :] = (dot_cols(pg, gw[f:, :]) * 0.125).astype(bf16)
        own = nets[rows, :]
        load[:f, :] += dot_rows(emb[rows, :], pg)
        load[f:2 * f, :] += dot_rows(agg[rows, :], pg)
        load[2 * f:3 * f, :] += dot_rows(own, vh) + dot_rows(own, vl)
        load[3 * f:4 * f, :] += dot_rows(own, ph) + dot_rows(own, plo)
        return 0

    lax.fori_loop(0, n // tile, step, 0)


def middle(sv, sp, nets, pre, embeds, aggregate, pair_w1, gnn_weight, small):
    n, f = nets.shape
    shape = jax.ShapeDtypeStruct
    return kernel_call(
        middle_body,
        (shape((n, f), f32), shape((n, f), bf16), shape((4 * f + 8, f), f32)),
        [vmem()] * 9, [], None, "middle",
    )(sv, sp, nets, pre, embeds, aggregate, pair_w1, gnn_weight, small)


def tail_body(n_region, n_dom, words, ag, base, hs, load, out, sums, extra,
              outgoing, ret, acc, r0, s0, r1, s1, r2, e0, ea, e1, eb, e2,
              hsend, hrecv, send0, recv0, send1, recv1, send2, recv2,
              gsend0, grecv0, gsend1, grecv1, gsend2, grecv2, es0, er0, es1, er1, es2, er2):
    place = Place(n_region, n_dom)
    n_chip, per = place.n_chip, place.per
    n, f = ag.shape
    halo = hs.shape[1]
    width = words.shape[1]
    rows = sums.shape[0]
    q0 = rows // 2
    q1 = q0 // n_chip
    q2 = q1 // n_dom
    core, chip, dom = place.core, place.chip, place.dom
    twin = place.at_region(chip * 2 + 1 - core)
    chips = [place.at_region(lax.rem(chip + k, n_chip) * 2 + core) for k in range(1, n_chip)]
    doms = [place.at_dom(place.dom_to(k)) for k in range(1, n_dom)]
    greet([twin] + chips + doms)

    c0 = [
        remote(load.at[pl.ds((1 - core) * q0, q0)], r0, send0, recv0, twin),
        remote(load.at[pl.ds(rows, 8)], e0, es0, er0, twin),
    ]
    for copy in c0:
        copy.start()

    def halo_copy(i, j):
        field, sub = place.field_to(i), place.sub_to(j)
        return remote(outgoing.at[field * per + sub], ret.at[dom],
                      hsend.at[i * per + j], hrecv.at[i * per + j], place.at_dom(field * per + sub))

    for i in range(HALF):
        field = place.field_to(i)
        part = dot_rows(counts_of(words[...], field + HALF), ag[...]).astype(bf16)
        for s in range(per):
            outgoing[field * per + s] = part[s * halo:(s + 1) * halo]
        for j in range(per):
            if i or j:
                halo_copy(i, j).start()
    ret[dom] = outgoing[dom]

    def own_field(field):
        part = slice(field * width, (field + 1) * width)
        acc[part, :] = base[part, :] + dot_rows(counts_of(words[...], field), ag[...])

    for copy in c0:
        copy.wait()
    s0[...] = load[pl.ds(core * q0, q0), :] + r0[...]
    ea[...] = load[pl.ds(rows, 8), :] + e0[...]
    c1 = []
    for k in range(1, n_chip):
        peer = lax.rem(chip + k, n_chip)
        c1.append(remote(s0.at[pl.ds(peer * q1, q1)], r1.at[k - 1], send1.at[k - 1], recv1.at[k - 1], chips[k - 1]))
        c1.append(remote(ea, e1.at[k - 1], es1.at[k - 1], er1.at[k - 1], chips[k - 1]))
    for copy in c1:
        copy.start()
    own_field(0)
    own_field(1)
    for copy in c1:
        copy.wait()
    total = s0[pl.ds(chip * q1, q1), :]
    etotal = ea[...]
    for k in range(1, n_chip):
        total = total + r1[k - 1]
        etotal = etotal + e1[k - 1]
    s1[...] = total
    eb[...] = etotal
    c2 = []
    for k in range(1, n_dom):
        peer = place.dom_to(k)
        c2.append(remote(s1.at[pl.ds(peer * q2, q2)], r2.at[k - 1], send2.at[k - 1], recv2.at[k - 1], doms[k - 1]))
        c2.append(remote(eb, e2.at[k - 1], es2.at[k - 1], er2.at[k - 1], doms[k - 1]))
    for copy in c2:
        copy.start()
    own_field(2)
    own_field(3)
    for copy in c2:
        copy.wait()
    total = s1[pl.ds(dom * q2, q2), :]
    etotal = eb[...]
    for k in range(1, n_dom):
        total = total + r2[k - 1]
        etotal = etotal + e2[k - 1]
    live = etotal[2:3, :]
    root = 8.0 / jnp.sqrt(live)
    mine = core * q0 + chip * q1 + dom * q2
    sums[pl.ds(mine, q2), :] = total * root
    extra[0:1, :] = etotal[0:1, :] * root
    extra[1:8, :] = jnp.broadcast_to(etotal[1:2, :] / live, (7, f))
    scale = 8.0 * (n * n_region * n_dom) / live

    block = sums.at[pl.ds(mine, q2)]
    g2 = [remote(block, block, gsend2.at[k - 1], grecv2.at[k - 1], doms[k - 1]) for k in range(1, n_dom)]
    for copy in g2:
        copy.start()

    for i in range(HALF):
        for j in range(per):
            if i or j:
                halo_copy(i, j).wait()
    tile = 512

    def final_step(t, _):
        part = rows_at(t, tile)
        total = acc[part, :]
        for field in range(HALF):
            ids = jnp.concatenate([hs[p:p + 1, :] for p in range(field * per, (field + 1) * per)], 1)
            got = ret[field * per:(field + 1) * per].reshape(per * halo, f)
            total = total + dot(row_hot(t * tile, tile, ids), got)
        out[part, :] = (total * scale).astype(bf16)
        return 0

    half_tiles = n // tile // 2
    lax.fori_loop(0, half_tiles, final_step, 0)
    for copy in g2:
        copy.wait()
    block = sums.at[pl.ds(core * q0 + chip * q1, q1)]
    g1 = [remote(block, block, gsend1.at[k - 1], grecv1.at[k - 1], chips[k - 1]) for k in range(1, n_chip)]
    for copy in g1:
        copy.start()
    lax.fori_loop(half_tiles, n // tile, final_step, 0)
    for copy in g1:
        copy.wait()
    block = sums.at[pl.ds(core * q0, q0)]
    g0 = remote(block, block, gsend0, grecv0, twin)
    g0.start()
    g0.wait()


def tail(n_region, n_dom, words, agg_grad, base, halo_send, load):
    n, f = agg_grad.shape
    peers, halo = halo_send.shape
    rows = load.shape[0] - 8
    n_chip = n_region // 2
    q0 = rows // 2
    q1 = q0 // n_chip
    q2 = q1 // n_dom
    sem = pltpu.SemaphoreType.DMA
    vm = lambda *dims: pltpu.VMEM(dims, f32)
    blocks = pltpu.VMEM((peers, halo, f), bf16)
    shape = jax.ShapeDtypeStruct
    pairs = [sem, sem, sem((n_chip - 1,)), sem((n_chip - 1,)), sem((n_dom - 1,)), sem((n_dom - 1,))]
    return kernel_call(
        functools.partial(tail_body, n_region, n_dom),
        (shape((n, f), bf16), shape((rows, f), f32), shape((8, f), f32)),
        [vmem()] * 5,
        [
            blocks, blocks, vm(n, f), vm(q0, f), vm(q0, f), vm(n_chip - 1, q1, f), vm(q1, f),
            vm(n_dom - 1, q2, f), vm(8, f), vm(8, f), vm(n_chip - 1, 8, f), vm(8, f), vm(n_dom - 1, 8, f),
            sem((n_dom,)), sem((n_dom,)),
        ] + pairs * 3,
        3, "tail",
    )(words, agg_grad, base, halo_send, load)


def local(
    embeds, neighbours, halo_send, gnn_weight, pair_local, pair_remote, pair_count, targets, pair_w1, pair_w2
):
    f = embeds.shape[1]
    sizes = lax.axis_size("region"), lax.axis_size("dom")
    words, pre, aggregate, nets, asked = head(*sizes, embeds, neighbours, halo_send, pair_remote, gnn_weight)
    sv, sp, small = pair(*sizes, nets, asked, pair_local, targets, pair_count, pair_w1, pair_w2)
    base, agg_grad, load = middle(sv, sp, nets, pre, embeds, aggregate, pair_w1, gnn_weight, small)
    embeds_grad, sums, extra = tail(*sizes, words, agg_grad, base, halo_send, load)
    return embeds_grad, sums[: 2 * f], sums[2 * f :], extra[0], extra[1, 0]


def solution(mesh):
    both = P(("region", "dom"), None)
    in_specs = (both, both, both, P(), both, both, both, both, P(), P())
    out_specs = (both, P(), P(), P(), P())
    return jax.shard_map(local, mesh=mesh, in_specs=in_specs, out_specs=out_specs, check_vma=False)
```

time: 456 us -> 162 us (0.36)
  Pallas kernels: 0 us -> 155 us
  matrix products: 118 us -> 0 us
  waiting for transfers between devices: 104 us -> 0 us
  blocking collectives: 68 us -> 0 us
  other arithmetic: 63.1 us -> 0 us
  local copies, waits for them, and re-layouts: 49.6 us -> 6.97 us
  starting transfers between devices: 30.3 us -> 0 us
  between operations: 19.1 us -> 0.67 us
    pallas_call x0 -> x4, Pallas kernels: none -> 155 us  [the longest x1 56.5 us: pair(): kernel_call(functools.partial(pair_body, n_region, n_dom), (shape((n, h),...]
    dot_general x11 -> x0, matrix products: 118 us -> none  [the longest x1 50 us: local(): agg_sum = jnp.dot(adjacency, table, preferred_element_type=jnp.float32)]
    psum x1 -> x0, waiting for transfers between devices: 80.3 us -> none  [local(): lax.psum((grad_gnn, grad_w1, grad_w2, sq_local), ('region', 'dom'))]
    psum x1 -> x0, blocking collectives: 68 us -> none  [local(): total_count = lax.psum(local_count, ('region', 'dom'))]
    scatter-add x2 -> x0, other arithmetic: 50.8 us -> none  [the longest x1 26.2 us: local(): nets_grad.at[asked.reshape(-1)]]
    gather x2 -> x0, local copies, waits for them, and re-layouts: 34 us -> none  [the longest x1 17 us: local(): victim = nets[pair_local]]
    all_to_all x5 -> x0, starting transfers between devices: 30.3 us -> none  [the longest x1 7.9 us: local(): lax.all_to_all(outgoing, 'dom', split_axis=0, concat_axis=0, tiled=True)]
    all_to_all x5 -> x0, waiting for transfers between devices: 23.2 us -> none  [the longest x1 14.8 us: local(): lax.all_to_all(outgoing, 'dom', split_axis=0, concat_axis=0, tiled=True)]
  transfers between devices with their start and end apart: 6 -> 0, of which waited for: 3 -> 0; matrix products, arithmetic and copies ran while one was open for 13% -> 0% of each run, Pallas kernels for 0% -> 0%
where the time goes in v2:
time: 162 us
  Pallas kernels  155 us (96%)
  local copies, waits for them, and re-layouts  6.97 us (4%)
    pallas_call x1, Pallas kernels, pair(): kernel_call(functools.partial(pair_body, n_region, n_dom), (shape((n, h),...  56.5 us
    pallas_call x1, Pallas kernels, tail(): kernel_call(functools.partial(tail_body, n_region, n_dom), (shape((n, f),...  48.5 us
    pallas_call x1, Pallas kernels, head(): kernel_call(functools.partial(head_body, n_region, n_dom), (shape((n, wid...  36.4 us
    pallas_call x1, Pallas kernels, middle(): kernel_call(middle_body, (shape((n, f), f32), shape((n, f), bf16), shape(...  13.2 us
    slice x3, local copies, waits for them, and re-layouts, local(): return (embeds_grad, sums[:2 * f], sums[2 * f:], extra[0], extra[1, 0])  4.78 us

profile of v2, /device:TPU:1, one launch (start us, length us, event | category | flops | bytes accessed | tf_op | source)
XLA Modules:
  0.0 162.2 jit_solution(7581114979172071992)
XLA Ops:
  0.6 1.2 broadcast_in_dim.3.w2
  1.9 36.4 %head.1 = (s32[2048,512]{1,0:T(8,128)}, f32[2048,256]{1,0:T(8,128)}, bf16[2048,256]{1,0:T(8,128)(2,1)}, bf16[2048,256]{1,0:T(8,128)(2,1)}, s32[8,512]{1,0:T(8,128)}) custom-call(bf16[2048,256]{1,0:T(8,128)(2,1)} %emb.3, s32[8,2048]{1,0:T(8,128)} %bitcast.3, s32[16,128]{1,0:T(8,128)} %hs.3, s32[8,512]{1,0:T(8,128)} %pr.1, bf16[512,256]{1,0:T(8,128)(2,1)} %gw.3), custom_call_target="tpu_custom_call" | custom-call | tf_op jit(solution)/shard_map/head/pallas_call | solution.py:216
  38.3 56.5 %pair.1 = (f32[2048,256]{1,0:T(8,128)}, f32[2048,256]{1,0:T(8,128)}, f32[8,256]{1,0:T(8,128)}) custom-call(bf16[2048,256]{1,0:T(8,128)(2,1)} %get-tuple-element.20.nets, s32[8,512]{1,0:T(8,128)} %get-tuple-element.21.asked, s32[8,512]{1,0:T(8,128)} %loc.1, f32[8,512]{1,0:T(8,128)} %tgt.1, s32[1,8]{1,0:T(1,128)} %cnt.1, bf16[512,256]{1,0:T(8,128)(2,1)} %w1.3, ...), custom_call_target="tpu_custom_call" | custom-call | tf_op jit(solution)/shard_map/pair/pallas_call | solution.py:340
  94.8 13.2 %middle.1 = (f32[2048,256]{1,0:T(8,128)}, bf16[2048,256]{1,0:T(8,128)(2,1)}, f32[1032,256]{1,0:T(8,128)}) custom-call(f32[2048,256]{1,0:T(8,128)} %get-tuple-element.22.sv, f32[2048,256]{1,0:T(8,128)} %get-tuple-element.23.sp, bf16[2048,256]{1,0:T(8,128)(2,1)} %get-tuple-element.20.nets, f32[2048,256]{1,0:T(8,128)} %get-tuple-element.24.pre, ...), custom_call_target="tpu_custom_call" | custom-call | tf_op jit(solution)/shard_map/middle/pallas_call | solution.py:377
  107.9 48.5 %tail.1 = (bf16[2048,256]{1,0:T(8,128)(2,1)}, f32[1024,256]{1,0:T(8,128)}, f32[8,256]{1,0:T(8,128)}) custom-call(s32[2048,512]{1,0:T(8,128)} %get-tuple-element.19.words, bf16[2048,256]{1,0:T(8,128)(2,1)} %get-tuple-element.27.ag, f32[2048,256]{1,0:T(8,128)} %get-tuple-element.28.base, s32[16,128]{1,0:T(8,128)} %hs.3, f32[1032,256]{1,0:T(8,128)} %get-tuple-element.29.load), custom_call_target="tpu_custom_call" | custom-call | tf_op jit(solution)/shard_map/tail/pallas_call | solution.py:526
  156.4 0.0 copy-start
  156.4 1.3 slice.15
  157.7 1.3 slice.14
  159.0 2.2 %fusion = (f32[512,256]{1,0:T(8,128)}, f32[512,256]{1,0:T(8,128)}) fusion(f32[1024,256]{1,0:T(8,128)} %get-tuple-element.31), kind=kLoop, calls=%fused_computation | loop fusion | bytes 2097152 | tf_op jit(solution)/shard_map/slice | solution.py:548
  161.2 0.0 copy-done
  161.2 1.0 copy.16
Async XLA Ops:
  156.4 4.8 %copy-start = (bf16[2048,256]{1,0:T(8,128)(2,1)S(1)}, bf16[2048,256]{1,0:T(8,128)(2,1)}, u32[]{:S(2)}) copy-start(bf16[2048,256]{1,0:T(8,128)(2,1)} %get-tuple-element.40) | copy-start | bytes 3145732

commit v3 on v2

v3 whole, which is shorter than its diff:
```python
import functools
import jax
import jax.numpy as jnp
from jax import lax
from jax.experimental import pallas as pl
from jax.experimental.pallas import tpu as pltpu
from jax.sharding import PartitionSpec as P

f32 = jnp.float32
bf16 = jnp.bfloat16
gelu_coef = 0.7978845608
contract_rows = (((0,), (0,)), ((), ()))
contract_cols = (((1,), (1,)), ((), ()))
VMEM_LIMIT = 62 * 1024 * 1024
MESH = pl.DeviceIdType.MESH
FIELDS = 8
HALF = FIELDS // 2
HEAD_TILE = 512


def gelu_both(value):
    inner = jnp.tanh(gelu_coef * (value + 0.044715 * value * value * value))
    half = 0.5 * (1.0 + inner)
    slope = half + 0.5 * value * (1.0 - inner * inner) * gelu_coef * (
        1.0 + 3.0 * 0.044715 * value * value
    )
    return value * half, slope


def dot(a, b):
    return jnp.dot(a, b, preferred_element_type=f32)


def dot_rows(a, b):
    return lax.dot_general(a, b, contract_rows, preferred_element_type=f32)


def dot_cols(a, b):
    return lax.dot_general(a, b, contract_cols, preferred_element_type=f32)


def split(value):
    high = value.astype(bf16)
    return high, (value - high.astype(f32)).astype(bf16)


def rows_at(i, tile):
    return pl.ds(pl.multiple_of(i * tile, tile), tile)


def lane_hot(ids, n):
    return (ids == lax.broadcasted_iota(jnp.int32, (ids.shape[0], n), 1)).astype(f32).astype(bf16)


def row_hot(base, tile, ids):
    row = lax.broadcasted_iota(jnp.int32, (tile, ids.shape[1]), 0)
    return (row == ids - base).astype(f32).astype(bf16)


def counts_of(words, field):
    return ((words >> (4 * field)) & 15).astype(f32).astype(bf16)


class Place:
    def __init__(self, n_region, n_dom):
        self.n_region, self.n_dom = n_region, n_dom
        self.n_chip = n_region // 2
        self.per = n_dom // HALF
        self.region = lax.axis_index("region")
        self.dom = lax.axis_index("dom")
        self.chip = self.region // 2
        self.core = lax.rem(self.region, 2)

    def region_to(self, m):
        chip = lax.rem(self.chip + lax.rem(m, self.n_chip), self.n_chip)
        return chip * 2 + lax.rem(self.core + m // self.n_chip, 2)

    def region_from(self, m):
        chip = lax.rem(self.chip + self.n_chip - lax.rem(m, self.n_chip), self.n_chip)
        return chip * 2 + lax.rem(self.core + m // self.n_chip, 2)

    def field_to(self, i):
        return lax.rem(self.dom // self.per + i, HALF)

    def sub_to(self, j):
        return lax.rem(lax.rem(self.dom, self.per) + j, self.per)

    def dom_to(self, k):
        return lax.rem(self.dom + k, self.n_dom)

    def at_region(self, r):
        return (r, self.dom)

    def at_dom(self, d):
        return (self.region, d)


def remote(src, dst, ssem, rsem, device):
    return pltpu.make_async_remote_copy(
        src_ref=src, dst_ref=dst, send_sem=ssem, recv_sem=rsem, device_id=device, device_id_type=MESH
    )


def vmem():
    return pl.BlockSpec(memory_space=pltpu.VMEM)


def smem():
    return pl.BlockSpec(memory_space=pltpu.SMEM)


def kernel_call(body, outs, in_specs, scratch, collective, name, out_specs=None):
    single = not isinstance(outs, tuple)
    specs = vmem() if single else tuple(vmem() for _ in outs)
    params = dict(vmem_limit_bytes=VMEM_LIMIT)
    if collective is not None:
        params.update(collective_id=collective, has_side_effects=True)
    return pl.pallas_call(
        body, out_shape=outs, in_specs=in_specs, out_specs=specs, scratch_shapes=scratch, name=name,
        compiler_params=pltpu.CompilerParams(**params),
    )


def gather_chunk(ids, table, n):
    return dot(lane_hot(ids.T, n), table[...]).astype(bf16)


def step_body(n_region, n_dom, emb, nb, hs, pr, gw, loc, tgt, cnt, w1, w2, out, sums, extra,
              words, wordst, pre, agg, nets, asked, own, hout, recv,
              outgoing, partner, grad, back, va, sv, sp, load, ag, hback, ret,
              r0, s0, r1, s1, r2, e0, ea, e1, eb, e2,
              hsend, hrecv, asend, arecv, fsend, frecv, bsend, brecv, tsend, trecv,
              send0, recv0, send1, recv1, send2, recv2,
              gsend0, grecv0, gsend1, grecv1, gsend2, grecv2, es0, er0, es1, er1, es2, er2):
    place = Place(n_region, n_dom)
    per, n_chip = place.per, place.n_chip
    me, dom, chip, core = place.region, place.dom, place.chip, place.core
    n, f = emb.shape
    h = w1.shape[1]
    halo = hs.shape[1]
    count = loc.shape[1]
    width = words.shape[1]
    wbits = width.bit_length() - 1
    others = ([place.at_dom(place.dom_to(k)) for k in range(1, n_dom)]
              + [place.at_region(place.region_to(m)) for m in range(1, n_region)])
    barrier = pltpu.get_barrier_semaphore()
    for device in others:
        pl.semaphore_signal(barrier, inc=1, device_id=device, device_id_type=MESH)

    def ask(m):
        r = place.region_to(m)
        return remote(pr.at[pl.ds(r, 1)], asked.at[pl.ds(me, 1)], asend.at[m], arecv.at[m], place.at_region(r))

    def halo_copy(i, j):
        p = place.field_to(i) * per + place.sub_to(j)
        return remote(hout.at[p], recv.at[dom], hsend.at[i * per + j], hrecv.at[i * per + j], place.at_dom(p))

    def back_halo(i, j):
        p = place.field_to(i) * per + place.sub_to(j)
        return remote(hback.at[p], ret.at[dom], tsend.at[i * per + j], trecv.at[i * per + j], place.at_dom(p))

    far = [(i, j) for i in range(HALF) for j in range(per) if i or j]

    for i in range(HALF):
        field = place.field_to(i)
        ids = jnp.concatenate([hs[pl.ds(field * per + s, 1), :] for s in range(per)], 1)
        rows = gather_chunk(ids, emb, n)
        for s in range(per):
            hout[field * per + s] = rows[s * halo:(s + 1) * halo]
        if i == 0:
            pl.semaphore_wait(barrier, len(others))
            for m in range(1, n_region):
                ask(m).start()
        for a, b in far:
            if a == i:
                halo_copy(a, b).start()
    recv[dom] = hout[dom]
    asked[pl.ds(me, 1), :] = pr[pl.ds(me, 1), :]

    tile = HEAD_TILE

    def own_step(t, _):
        rows = rows_at(t, tile)
        ids = nb[:, rows].T
        low = ids & (width - 1)
        weight = jnp.left_shift(1, 4 * (ids >> wbits))
        lane = lax.broadcasted_iota(jnp.int32, (tile, width), 1)
        word = jnp.zeros((tile, width), jnp.int32)
        for d in range(ids.shape[1]):
            word = word + jnp.where(lane == low[:, d:d + 1], weight[:, d:d + 1], 0)
        words[rows, :] = word
        acc = jnp.zeros((tile, f), f32)
        for field in range(HALF):
            acc = acc + dot(counts_of(word, field), emb[field * width:(field + 1) * width, :])
        own[rows, :] = acc
        return 0

    lax.fori_loop(0, n // tile, own_step, 0)
    for a, b in far:
        halo_copy(a, b).wait()

    def halo_step(t, _):
        rows = rows_at(t, tile)
        word = words[rows, :]
        acc = own[rows, :]
        for field in range(HALF):
            table = recv[field * per:(field + 1) * per].reshape(width, f)
            acc = acc + dot(counts_of(word, field + HALF), table)
        mean = (acc * 0.125).astype(bf16)
        mine = emb[rows, :]
        lin = dot(mine, gw[:f, :]) + dot(mean, gw[f:, :])
        pre[rows, :] = lin
        agg[rows, :] = mean
        nets[rows, :] = (mine.astype(f32) + gelu_both(lin)[0]).astype(bf16)
        return 0

    lax.fori_loop(0, n // tile, halo_step, 0)
    for m in range(1, n_region):
        ask(m).wait()

    def out_copy(m):
        r = place.region_to(m)
        return remote(outgoing.at[r], partner.at[me], fsend.at[m], frecv.at[m], place.at_region(r))

    def back_copy(m):
        r = place.region_from(m)
        return remote(grad.at[r], back.at[me], bsend.at[m], brecv.at[m], place.at_region(r))

    def gather_step(m, _):
        r = place.region_to(m)
        outgoing[r] = gather_chunk(asked[pl.ds(r, 1), :], nets, n)
        out_copy(m).start()
        return 0

    lax.fori_loop(1, n_region, gather_step, 0)
    partner[me] = gather_chunk(asked[pl.ds(me, 1), :], nets, n)

    def victim_step(q, _):
        va[q] = dot(gather_chunk(loc[pl.ds(q, 1), :], nets, n), w1[:f, :])
        return 0

    lax.fori_loop(0, n_region, victim_step, 0)
    w2f = w2[...].astype(f32).reshape(1, h)
    w2mat = jnp.broadcast_to(w2f, (h, h)).T.astype(bf16)

    rows4 = 4 * f
    load[rows4:, :] = jnp.zeros((8, h), f32)
    live_count = cnt[0, 0]
    for q in range(1, n_region):
        live_count = live_count + cnt[0, q]
    load[rows4 + 2:rows4 + 3, :] = jnp.zeros((1, h), f32) + live_count.astype(f32)

    def pair_step(m):
        q = place.region_from(m)
        linear = va[q] + dot(partner[q], w1[f:, :])
        act, slope = gelu_both(linear)
        act = act.astype(bf16)
        scores = dot(act, w2mat)
        target = tgt[pl.ds(q, 1), :].T
        live = lax.broadcasted_iota(jnp.int32, (count, 1), 0) < cnt[0, q]
        errors = jnp.where(live, scores - target, 0.0)
        residual = 2.0 * errors
        grad[q] = (residual * w2f * slope).astype(bf16)
        load[rows4:rows4 + 1, :] += jnp.sum(residual * act.astype(f32), axis=0, keepdims=True)
        load[rows4 + 1:rows4 + 2, :] += jnp.sum(errors * errors, axis=0, keepdims=True)

    pair_step(0)

    def away_step(m, _):
        out_copy(m).wait_recv()
        pair_step(m)
        back_copy(m).start()
        return 0

    lax.fori_loop(1, n_region, away_step, 0)
    big = 512

    def victim_scatter(t, _):
        total = jnp.zeros((big, h), f32)
        for q in range(n_region):
            total = total + dot(row_hot(t * big, big, loc[q:q + 1, :]), grad[q])
        sv[rows_at(t, big), :] = total
        sp[rows_at(t, big), :] = dot(row_hot(t * big, big, asked[pl.ds(me, 1), :]), grad[me])
        return 0

    lax.fori_loop(0, n // big, victim_scatter, 0)

    def turn(t, _):
        rows = rows_at(t, 256)
        wordst[:, rows] = words[rows, :].T
        return 0

    lax.fori_loop(0, n // 256, turn, 0)

    def partner_scatter(m, _):
        r = place.region_to(m)
        back_copy(m).wait_recv()
        ids = asked[pl.ds(r, 1), :]
        rows_back = back[r]
        for t in range(n // big):
            sp[t * big:(t + 1) * big, :] += dot(row_hot(t * big, big, ids), rows_back)
        return 0

    lax.fori_loop(1, n_region, partner_scatter, 0)

    load[:rows4, :] = jnp.zeros((rows4, f), f32)

    def middle_step(t, _):
        rows = rows_at(t, tile)
        vh, vl = split(sv[rows, :])
        ph, plo = split(sp[rows, :])
        ng = dot_cols(vh, w1[:f, :]) + dot_cols(vl, w1[:f, :]) + dot_cols(ph, w1[f:, :]) + dot_cols(plo, w1[f:, :])
        pg = (ng * gelu_both(pre[rows, :])[1]).astype(bf16)
        own[rows, :] = ng + dot_cols(pg, gw[:f, :])
        ag[rows, :] = (dot_cols(pg, gw[f:, :]) * 0.125).astype(bf16)
        mine = nets[rows, :]
        load[:f, :] += dot_rows(emb[rows, :], pg)
        load[f:2 * f, :] += dot_rows(agg[rows, :], pg)
        load[2 * f:3 * f, :] += dot_rows(mine, vh) + dot_rows(mine, vl)
        load[3 * f:4 * f, :] += dot_rows(mine, ph) + dot_rows(mine, plo)
        return 0

    lax.fori_loop(0, n // tile, middle_step, 0)

    q0 = rows4 // 2
    q1 = q0 // n_chip
    q2 = q1 // n_dom
    twin = place.at_region(chip * 2 + 1 - core)
    chips = [place.at_region(lax.rem(chip + k, n_chip) * 2 + core) for k in range(1, n_chip)]
    doms = [place.at_dom(place.dom_to(k)) for k in range(1, n_dom)]
    c0 = [
        remote(load.at[pl.ds((1 - core) * q0, q0)], r0, send0, recv0, twin),
        remote(load.at[pl.ds(rows4, 8)], e0, es0, er0, twin),
    ]
    for copy in c0:
        copy.start()

    for i in range(HALF):
        field = place.field_to(i)
        part = dot(counts_of(wordst[...], field + HALF), ag[...]).astype(bf16)
        for s in range(per):
            hback[field * per + s] = part[s * halo:(s + 1) * halo]
        for a, b in far:
            if a == i:
                back_halo(a, b).start()
    ret[dom] = hback[dom]

    def own_field(field):
        part = slice(field * width, (field + 1) * width)
        own[part, :] = own[part, :] + dot(counts_of(wordst[...], field), ag[...])

    for copy in c0:
        copy.wait()
    s0[...] = load[pl.ds(core * q0, q0), :] + r0[...]
    ea[...] = load[pl.ds(rows4, 8), :] + e0[...]
    c1 = []
    for k in range(1, n_chip):
        peer = lax.rem(chip + k, n_chip)
        c1.append(remote(s0.at[pl.ds(peer * q1, q1)], r1.at[k - 1], send1.at[k - 1], recv1.at[k - 1], chips[k - 1]))
        c1.append(remote(ea, e1.at[k - 1], es1.at[k - 1], er1.at[k - 1], chips[k - 1]))
    for copy in c1:
        copy.start()
    own_field(0)
    own_field(1)
    for copy in c1:
        copy.wait()
    total = s0[pl.ds(chip * q1, q1), :]
    etotal = ea[...]
    for k in range(1, n_chip):
        total = total + r1[k - 1]
        etotal = etotal + e1[k - 1]
    s1[...] = total
    eb[...] = etotal
    c2 = []
    for k in range(1, n_dom):
        peer = place.dom_to(k)
        c2.append(remote(s1.at[pl.ds(peer * q2, q2)], r2.at[k - 1], send2.at[k - 1], recv2.at[k - 1], doms[k - 1]))
        c2.append(remote(eb, e2.at[k - 1], es2.at[k - 1], er2.at[k - 1], doms[k - 1]))
    for copy in c2:
        copy.start()
    own_field(2)
    own_field(3)
    for copy in c2:
        copy.wait()
    total = s1[pl.ds(dom * q2, q2), :]
    etotal = eb[...]
    for k in range(1, n_dom):
        total = total + r2[k - 1]
        etotal = etotal + e2[k - 1]
    live = etotal[2:3, :]
    root = 8.0 / jnp.sqrt(live)
    mine = core * q0 + chip * q1 + dom * q2
    sums[pl.ds(mine, q2), :] = total * root
    extra[0:1, :] = etotal[0:1, :] * root
    extra[1:8, :] = jnp.broadcast_to(etotal[1:2, :] / live, (7, f))
    scale = 8.0 * (n * n_region * n_dom) / live

    block = sums.at[pl.ds(mine, q2)]
    g2 = [remote(block, block, gsend2.at[k - 1], grecv2.at[k - 1], doms[k - 1]) for k in range(1, n_dom)]
    for copy in g2:
        copy.start()
    for copy in g2:
        copy.wait()
    block1 = sums.at[pl.ds(core * q0 + chip * q1, q1)]
    g1 = [remote(block1, block1, gsend1.at[k - 1], grecv1.at[k - 1], chips[k - 1]) for k in range(1, n_chip)]
    for copy in g1:
        copy.start()
    for a, b in far:
        back_halo(a, b).wait()

    def final_step(t, _):
        part = rows_at(t, big)
        total = own[part, :]
        for field in range(HALF):
            ids = jnp.concatenate([hs[p:p + 1, :] for p in range(field * per, (field + 1) * per)], 1)
            got = ret[field * per:(field + 1) * per].reshape(per * halo, f)
            total = total + dot(row_hot(t * big, big, ids), got)
        out[part, :] = (total * scale).astype(bf16)
        return 0

    lax.fori_loop(0, n // big, final_step, 0)
    for copy in g1:
        copy.wait()
    block0 = sums.at[pl.ds(core * q0, q0)]
    g0 = remote(block0, block0, gsend0, grecv0, twin)
    g0.start()

    def drain(m, _):
        out_copy(m).wait_send()
        back_copy(m).wait_send()
        return 0

    lax.fori_loop(1, n_region, drain, 0)
    g0.wait()


def train_step(n_region, n_dom, emb, nb, hs, pr, gw, loc, tgt, cnt, w1, w2):
    n, f = emb.shape
    h = w1.shape[1]
    peers, halo = hs.shape
    regions, slots = loc.shape
    width = 2 * n // FIELDS
    rows = 4 * f
    n_chip = n_region // 2
    q0 = rows // 2
    q1 = q0 // n_chip
    q2 = q1 // n_dom
    sem = pltpu.SemaphoreType.DMA
    vm = lambda *dims: pltpu.VMEM(dims, f32)
    vb = lambda *dims: pltpu.VMEM(dims, bf16)
    vi = lambda *dims: pltpu.VMEM(dims, jnp.int32)
    shape = jax.ShapeDtypeStruct
    sums_sems = [sem, sem, sem((n_chip - 1,)), sem((n_chip - 1,)), sem((n_dom - 1,)), sem((n_dom - 1,))]
    return kernel_call(
        functools.partial(step_body, n_region, n_dom),
        (shape((n, f), bf16), shape((rows, f), f32), shape((8, f), f32)),
        [vmem()] * 7 + [smem()] + [vmem()] * 2,
        [
            vi(n, width), vi(width, n), vm(n, f), vb(n, f), vb(n, f), vi(regions, slots), vm(n, f),
            vb(peers, halo, f), vb(peers, halo, f),
            vb(regions, slots, f), vb(regions, slots, f), vb(regions, slots, h), vb(regions, slots, h),
            vm(regions, slots, h), vm(n, h), vm(n, h), vm(rows + 8, f), vb(n, f),
            vb(peers, halo, f), vb(peers, halo, f),
            vm(q0, f), vm(q0, f), vm(n_chip - 1, q1, f), vm(q1, f), vm(n_dom - 1, q2, f),
            vm(8, f), vm(8, f), vm(n_chip - 1, 8, f), vm(8, f), vm(n_dom - 1, 8, f),
            sem((n_dom,)), sem((n_dom,)), sem((n_region,)), sem((n_region,)),
            sem((n_region,)), sem((n_region,)), sem((n_region,)), sem((n_region,)), sem((n_dom,)), sem((n_dom,)),
        ] + sums_sems * 3,
        1, "train_step",
    )(emb, nb.T, hs, pr, gw, loc, tgt, cnt, w1, w2)


def finish_body(grad, sums, extra, out, gnn, w1, w2, loss):
    half = gnn.shape[0]
    out[...] = grad[...]
    gnn[...] = sums[:half, :]
    w1[...] = sums[half:, :]
    w2[...] = extra[0:1, :].reshape(w2.shape)
    loss[...] = extra[1:2, 0:1]


def finish(grad, sums, extra):
    rows, f = sums.shape
    shape = jax.ShapeDtypeStruct
    return kernel_call(
        finish_body,
        (shape(grad.shape, bf16), shape((rows // 2, f), f32), shape((rows // 2, f), f32), shape((f,), f32),
         shape((1, 1), f32)),
        [vmem()] * 3, [], None, "finish",
    )(grad, sums, extra)


def local(
    embeds, neighbours, halo_send, gnn_weight, pair_local, pair_remote, pair_count, targets, pair_w1, pair_w2
):
    sizes = lax.axis_size("region"), lax.axis_size("dom")
    outs = train_step(
        *sizes, embeds, neighbours, halo_send, pair_remote, gnn_weight, pair_local, targets, pair_count,
        pair_w1, pair_w2
    )
    *grads, loss = finish(*outs)
    return *grads, loss.reshape(())


def solution(mesh):
    both = P(("region", "dom"), None)
    in_specs = (both, both, both, P(), both, both, both, both, P(), P())
    out_specs = (both, P(), P(), P(), P())
    return jax.shard_map(local, mesh=mesh, in_specs=in_specs, out_specs=out_specs, check_vma=False)
```

time: 162 us -> 134 us (0.83)
  Pallas kernels: 155 us -> 133 us
  local copies, waits for them, and re-layouts: 6.97 us -> 0 us
    pallas_call x4 -> x2, Pallas kernels: 155 us -> 133 us  [the longest x1 130 us: train_step(): kernel_call(functools.partial(step_body, n_region, n_dom), (shape((n, f),...]
    slice x3 -> x0, local copies, waits for them, and re-layouts: 4.78 us -> none  [local(): return (embeds_grad, sums[:2 * f], sums[2 * f:], extra[0], extra[1, 0])]
where the time goes in v3:
time: 134 us
  Pallas kernels  133 us (99%)
    pallas_call x1, Pallas kernels, train_step(): kernel_call(functools.partial(step_body, n_region, n_dom), (shape((n, f),...  130 us
    pallas_call x1, Pallas kernels, finish(): kernel_call(finish_body, (shape(grad.shape, bf16), shape((rows // 2, f),...  2.9 us

profile of v3, /device:TPU:1, one launch (start us, length us, event | category | flops | bytes accessed | tf_op | source)
XLA Modules:
  0.0 133.9 jit_solution(1975680692413277574)
XLA Ops:
  0.6 130.3 %train_step.1 = (bf16[2048,256]{1,0:T(8,128)(2,1)}, f32[1024,256]{1,0:T(8,128)}, f32[8,256]{1,0:T(8,128)}) custom-call(bf16[2048,256]{1,0:T(8,128)(2,1)} %emb.1, s32[8,2048]{1,0:T(8,128)} %bitcast.2, s32[16,128]{1,0:T(8,128)} %hs.1, s32[8,512]{1,0:T(8,128)} %pr.1, bf16[512,256]{1,0:T(8,128)(2,1)} %gw.1, s32[8,512]{1,0:T(8,128)} %loc.1, f32[8,512]{1,0:T(8,128)} %tgt.1, ...), custom_call_target="tpu_custom_call" | custom-call | tf_op jit(solution)/shard_map/train_step/pallas_call | solution.py:454
  131.0 2.9 %finish.1 = (bf16[2048,256]{1,0:T(8,128)(2,1)}, f32[512,256]{1,0:T(8,128)}, f32[512,256]{1,0:T(8,128)}, f32[256]{0:T(256)}, f32[1,1]{1,0:T(1,128)}) custom-call(bf16[2048,256]{1,0:T(8,128)(2,1)} %get-tuple-element.13.grad, f32[1024,256]{1,0:T(8,128)} %get-tuple-element.14.sums, f32[8,256]{1,0:T(8,128)} %get-tuple-element.15.extra), custom_call_target="tpu_custom_call" | custom-call | tf_op jit(solution)/shard_map/finish/pallas_call | solution.py:485

commit v4 on v3

--- a/solution.py
+++ b/solution.py
@@ -84,6 +84,9 @@
 
     def sub_to(self, j):
         return lax.rem(lax.rem(self.dom, self.per) + j, self.per)
+
+    def field_from(self, i):
+        return lax.rem(self.dom // self.per + HALF - i, HALF)
 
     def dom_to(self, k):
         return lax.rem(self.dom + k, self.n_dom)
@@ -167,13 +170,11 @@
         rows = gather_chunk(ids, emb, n)
         for s in range(per):
             hout[field * per + s] = rows[s * halo:(s + 1) * halo]
-        if i == 0:
-            pl.semaphore_wait(barrier, len(others))
-            for m in range(1, n_region):
-                ask(m).start()
-        for a, b in far:
-            if a == i:
-                halo_copy(a, b).start()
+    pl.semaphore_wait(barrier, len(others))
+    for m in range(1, n_region):
+        ask(m).start()
+    for a, b in far:
+        halo_copy(a, b).start()
     recv[dom] = hout[dom]
     asked[pl.ds(me, 1), :] = pr[pl.ds(me, 1), :]
 
@@ -196,16 +197,28 @@
         return 0
 
     lax.fori_loop(0, n // tile, own_step, 0)
-    for a, b in far:
-        halo_copy(a, b).wait()
+
+    def arrived(i):
+        for a, b in far:
+            if a == i:
+                halo_copy(a, b).wait()
+        field = place.field_from(i)
+        return field + HALF, recv[pl.ds(field * per, per)].reshape(width, f)
+
+    for i in range(HALF - 1):
+        field, table = arrived(i)
+
+        def field_step(t, _):
+            rows = rows_at(t, tile)
+            own[rows, :] += dot(counts_of(words[rows, :], field), table)
+            return 0
+
+        lax.fori_loop(0, n // tile, field_step, 0)
+    last_field, last_table = arrived(HALF - 1)
 
     def halo_step(t, _):
         rows = rows_at(t, tile)
-        word = words[rows, :]
-        acc = own[rows, :]
-        for field in range(HALF):
-            table = recv[field * per:(field + 1) * per].reshape(width, f)
-            acc = acc + dot(counts_of(word, field + HALF), table)
+        acc = own[rows, :] + dot(counts_of(words[rows, :], last_field), last_table)
         mean = (acc * 0.125).astype(bf16)
         mine = emb[rows, :]
         lin = dot(mine, gw[:f, :]) + dot(mean, gw[f:, :])
@@ -292,6 +305,17 @@
 
     lax.fori_loop(0, n // 256, turn, 0)
 
+    load[:rows4, :] = jnp.zeros((rows4, f), f32)
+
+    def victim_middle(t, _):
+        rows = rows_at(t, tile)
+        vh, vl = split(sv[rows, :])
+        sv[rows, :] = dot_cols(vh, w1[:f, :]) + dot_cols(vl, w1[:f, :])
+        load[2 * f:3 * f, :] += dot_rows(nets[rows, :], vh) + dot_rows(nets[rows, :], vl)
+        return 0
+
+    lax.fori_loop(0, n // tile, victim_middle, 0)
+
     def partner_scatter(m, _):
         r = place.region_to(m)
         back_copy(m).wait_recv()
@@ -303,20 +327,16 @@
 
     lax.fori_loop(1, n_region, partner_scatter, 0)
 
-    load[:rows4, :] = jnp.zeros((rows4, f), f32)
-
     def middle_step(t, _):
         rows = rows_at(t, tile)
-        vh, vl = split(sv[rows, :])
         ph, plo = split(sp[rows, :])
-        ng = dot_cols(vh, w1[:f, :]) + dot_cols(vl, w1[:f, :]) + dot_cols(ph, w1[f:, :]) + dot_cols(plo, w1[f:, :])
+        ng = sv[rows, :] + dot_cols(ph, w1[f:, :]) + dot_cols(plo, w1[f:, :])
         pg = (ng * gelu_both(pre[rows, :])[1]).astype(bf16)
         own[rows, :] = ng + dot_cols(pg, gw[:f, :])
         ag[rows, :] = (dot_cols(pg, gw[f:, :]) * 0.125).astype(bf16)
         mine = nets[rows, :]
         load[:f, :] += dot_rows(emb[rows, :], pg)
         load[f:2 * f, :] += dot_rows(agg[rows, :], pg)
-        load[2 * f:3 * f, :] += dot_rows(mine, vh) + dot_rows(mine, vl)
         load[3 * f:4 * f, :] += dot_rows(mine, ph) + dot_rows(mine, plo)
         return 0
 
@@ -328,43 +348,50 @@
     twin = place.at_region(chip * 2 + 1 - core)
     chips = [place.at_region(lax.rem(chip + k, n_chip) * 2 + core) for k in range(1, n_chip)]
     doms = [place.at_dom(place.dom_to(k)) for k in range(1, n_dom)]
+    chunk0 = [lax.rem(chip + k, n_chip) for k in range(n_chip)]
     c0 = [
-        remote(load.at[pl.ds((1 - core) * q0, q0)], r0, send0, recv0, twin),
-        remote(load.at[pl.ds(rows4, 8)], e0, es0, er0, twin),
+        remote(load.at[pl.ds((1 - core) * q0 + chunk0[k] * q1, q1)], r0.at[k], send0.at[k], recv0.at[k], twin)
+        for k in range(n_chip)
     ]
-    for copy in c0:
-        copy.start()
+    x0 = remote(load.at[pl.ds(rows4, 8)], e0, es0, er0, twin)
+    x0.start()
+    for k in list(range(1, n_chip)) + [0]:
+        c0[k].start()
 
     for i in range(HALF):
         field = place.field_to(i)
         part = dot(counts_of(wordst[...], field + HALF), ag[...]).astype(bf16)
         for s in range(per):
             hback[field * per + s] = part[s * halo:(s + 1) * halo]
-        for a, b in far:
-            if a == i:
-                back_halo(a, b).start()
+        if i < 2:
+            for a, b in far:
+                if a == i:
+                    back_halo(a, b).start()
     ret[dom] = hback[dom]
 
     def own_field(field):
         part = slice(field * width, (field + 1) * width)
         own[part, :] = own[part, :] + dot(counts_of(wordst[...], field), ag[...])
 
-    for copy in c0:
-        copy.wait()
-    s0[...] = load[pl.ds(core * q0, q0), :] + r0[...]
+    x0.wait()
     ea[...] = load[pl.ds(rows4, 8), :] + e0[...]
     c1 = []
     for k in range(1, n_chip):
-        peer = lax.rem(chip + k, n_chip)
-        c1.append(remote(s0.at[pl.ds(peer * q1, q1)], r1.at[k - 1], send1.at[k - 1], recv1.at[k - 1], chips[k - 1]))
-        c1.append(remote(ea, e1.at[k - 1], es1.at[k - 1], er1.at[k - 1], chips[k - 1]))
-    for copy in c1:
+        copy = remote(ea, e1.at[k - 1], es1.at[k - 1], er1.at[k - 1], chips[k - 1])
         copy.start()
-    own_field(0)
-    own_field(1)
+        c1.append(copy)
+    for k in list(range(1, n_chip)) + [0]:
+        c0[k].wait()
+        s0[k] = load[pl.ds(core * q0 + chunk0[k] * q1, q1), :] + r0[k]
+        if k:
+            copy = remote(s0.at[k], r1.at[k - 1], send1.at[k - 1], recv1.at[k - 1], chips[k - 1])
+            copy.start()
+            c1.append(copy)
+    for field in range(HALF):
+        own_field(field)
     for copy in c1:
         copy.wait()
-    total = s0[pl.ds(chip * q1, q1), :]
+    total = s0[0]
     etotal = ea[...]
     for k in range(1, n_chip):
         total = total + r1[k - 1]
@@ -378,8 +405,9 @@
         c2.append(remote(eb, e2.at[k - 1], es2.at[k - 1], er2.at[k - 1], doms[k - 1]))
     for copy in c2:
         copy.start()
-    own_field(2)
-    own_field(3)
+    for a, b in far:
+        if a == 2:
+            back_halo(a, b).start()
     for copy in c2:
         copy.wait()
     total = s1[pl.ds(dom * q2, q2), :]
@@ -389,22 +417,32 @@
         etotal = etotal + e2[k - 1]
     live = etotal[2:3, :]
     root = 8.0 / jnp.sqrt(live)
-    mine = core * q0 + chip * q1 + dom * q2
-    sums[pl.ds(mine, q2), :] = total * root
+    base = core * n_chip * n_dom
+    mine = base + chip * n_dom + dom
+    sums[mine] = (total * root).astype(bf16)
+    block = sums.at[pl.ds(mine, 1)]
+    g2 = [remote(block, block, gsend2.at[k - 1], grecv2.at[k - 1], doms[k - 1]) for k in range(1, n_dom)]
+    for copy in g2:
+        copy.start()
+    for a, b in far:
+        if a == 3:
+            back_halo(a, b).start()
     extra[0:1, :] = etotal[0:1, :] * root
     extra[1:8, :] = jnp.broadcast_to(etotal[1:2, :] / live, (7, f))
     scale = 8.0 * (n * n_region * n_dom) / live
-
-    block = sums.at[pl.ds(mine, q2)]
-    g2 = [remote(block, block, gsend2.at[k - 1], grecv2.at[k - 1], doms[k - 1]) for k in range(1, n_dom)]
-    for copy in g2:
-        copy.start()
     for copy in g2:
         copy.wait()
-    block1 = sums.at[pl.ds(core * q0 + chip * q1, q1)]
+    block1 = sums.at[pl.ds(base + chip * n_dom, n_dom)]
     g1 = [remote(block1, block1, gsend1.at[k - 1], grecv1.at[k - 1], chips[k - 1]) for k in range(1, n_chip)]
     for copy in g1:
         copy.start()
+
+    def across(k):
+        part = sums.at[pl.ds(base + lax.rem(chip + n_chip - k, n_chip) * n_dom, n_dom)]
+        return remote(part, part, gsend0.at[k], grecv0.at[k], twin)
+
+    g0 = [across(k) for k in range(n_chip)]
+    g0[0].start()
     for a, b in far:
         back_halo(a, b).wait()
 
@@ -419,11 +457,9 @@
         return 0
 
     lax.fori_loop(0, n // big, final_step, 0)
-    for copy in g1:
-        copy.wait()
-    block0 = sums.at[pl.ds(core * q0, q0)]
-    g0 = remote(block0, block0, gsend0, grecv0, twin)
-    g0.start()
+    for k in range(1, n_chip):
+        g1[k - 1].wait()
+        g0[k].start()
 
     def drain(m, _):
         out_copy(m).wait_send()
@@ -431,7 +467,8 @@
         return 0
 
     lax.fori_loop(1, n_region, drain, 0)
-    g0.wait()
+    for copy in g0:
+        copy.wait()
 
 
 def train_step(n_region, n_dom, emb, nb, hs, pr, gw, loc, tgt, cnt, w1, w2):
@@ -450,10 +487,10 @@
     vb = lambda *dims: pltpu.VMEM(dims, bf16)
     vi = lambda *dims: pltpu.VMEM(dims, jnp.int32)
     shape = jax.ShapeDtypeStruct
-    sums_sems = [sem, sem, sem((n_chip - 1,)), sem((n_chip - 1,)), sem((n_dom - 1,)), sem((n_dom - 1,))]
+    sums_sems = [sem((n_chip,)), sem((n_chip,)), sem((n_chip - 1,)), sem((n_chip - 1,)), sem((n_dom - 1,)), sem((n_dom - 1,))]
     return kernel_call(
         functools.partial(step_body, n_region, n_dom),
-        (shape((n, f), bf16), shape((rows, f), f32), shape((8, f), f32)),
+        (shape((n, f), bf16), shape((rows // q2, q2, f), bf16), shape((8, f), f32)),
         [vmem()] * 7 + [smem()] + [vmem()] * 2,
         [
             vi(n, width), vi(width, n), vm(n, f), vb(n, f), vb(n, f), vi(regions, slots), vm(n, f),
@@ -461,26 +498,27 @@
             vb(regions, slots, f), vb(regions, slots, f), vb(regions, slots, h), vb(regions, slots, h),
             vm(regions, slots, h), vm(n, h), vm(n, h), vm(rows + 8, f), vb(n, f),
             vb(peers, halo, f), vb(peers, halo, f),
-            vm(q0, f), vm(q0, f), vm(n_chip - 1, q1, f), vm(q1, f), vm(n_dom - 1, q2, f),
+            vm(n_chip, q1, f), vm(n_chip, q1, f), vm(n_chip - 1, q1, f), vm(q1, f), vm(n_dom - 1, q2, f),
             vm(8, f), vm(8, f), vm(n_chip - 1, 8, f), vm(8, f), vm(n_dom - 1, 8, f),
             sem((n_dom,)), sem((n_dom,)), sem((n_region,)), sem((n_region,)),
             sem((n_region,)), sem((n_region,)), sem((n_region,)), sem((n_region,)), sem((n_dom,)), sem((n_dom,)),
-        ] + sums_sems * 3,
+        ] + sums_sems * 2 + [sem, sem] + sums_sems[2:],
         1, "train_step",
     )(emb, nb.T, hs, pr, gw, loc, tgt, cnt, w1, w2)
 
 
 def finish_body(grad, sums, extra, out, gnn, w1, w2, loss):
-    half = gnn.shape[0]
+    half = sums.shape[0] // 2
     out[...] = grad[...]
-    gnn[...] = sums[:half, :]
-    w1[...] = sums[half:, :]
+    gnn[...] = sums[:half].reshape(gnn.shape).astype(f32)
+    w1[...] = sums[half:].reshape(w1.shape).astype(f32)
     w2[...] = extra[0:1, :].reshape(w2.shape)
     loss[...] = extra[1:2, 0:1]
 
 
 def finish(grad, sums, extra):
-    rows, f = sums.shape
+    f = sums.shape[2]
+    rows = sums.shape[0] * sums.shape[1]
     shape = jax.ShapeDtypeStruct
     return kernel_call(
         finish_body,

time: 134 us -> 125 us (0.933); the launches traced: 134 us -> 123 us
  Pallas kernels: 133 us -> 123 us
    pallas_call x1, Pallas kernels: 130 us -> 120 us  [train_step(): kernel_call(functools.partial(step_body, n_region, n_dom), (shape((n, f),...]
where the time goes in v4:
time: 125 us; the launch traced here: 123 us
  Pallas kernels  123 us (98%)
    pallas_call x1, Pallas kernels, train_step(): kernel_call(functools.partial(step_body, n_region, n_dom), (shape((n, f),...  120 us
    pallas_call x1, Pallas kernels, finish(): kernel_call(finish_body, (shape(grad.shape, bf16), shape((rows // 2, f),...  2.75 us

profile of v4, /device:TPU:1, one launch (start us, length us, event | category | flops | bytes accessed | tf_op | source)
XLA Modules:
  0.0 123.4 jit_solution(12413318105235085542)
XLA Ops:
  0.6 120.0 %train_step.1 = (bf16[2048,256]{1,0:T(8,128)(2,1)}, bf16[128,8,256]{2,1,0:T(8,128)(2,1)}, f32[8,256]{1,0:T(8,128)}) custom-call(bf16[2048,256]{1,0:T(8,128)(2,1)} %emb.1, s32[8,2048]{1,0:T(8,128)} %bitcast.2, s32[16,128]{1,0:T(8,128)} %hs.1, s32[8,512]{1,0:T(8,128)} %pr.1, bf16[512,256]{1,0:T(8,128)(2,1)} %gw.1, s32[8,512]{1,0:T(8,128)} %loc.1, ...), custom_call_target="tpu_custom_call" | custom-call | tf_op jit(solution)/shard_map/train_step/pallas_call | solution.py:491
  120.6 2.8 %finish.1 = (bf16[2048,256]{1,0:T(8,128)(2,1)}, f32[512,256]{1,0:T(8,128)}, f32[512,256]{1,0:T(8,128)}, f32[256]{0:T(256)}, f32[1,1]{1,0:T(1,128)}) custom-call(bf16[2048,256]{1,0:T(8,128)(2,1)} %get-tuple-element.13.grad, bf16[128,8,256]{2,1,0:T(8,128)(2,1)} %get-tuple-element.14.sums, f32[8,256]{1,0:T(8,128)} %get-tuple-element.15.extra), custom_call_target="tpu_custom_call" | custom-call | tf_op jit(solution)/shard_map/finish/pallas_call | solution.py:523
